TPU v7x, 256 devices: a whole 4x4x8 slice. The times are simulated.
256 devices in a mesh: dp: 4 (over y_lo, core), space: 64 (over z, y_hi, x).
Axes of the slice: x: 4, y: 4 (y_hi: 2, y_lo: 2; y = y_hi * 2 + y_lo), z: 8, core: 2. Of those that a mesh axis runs over, the one named last changes fastest.
Arguments:
- inputs: bfloat16 [12, 64, 4, 8192], P('dp', 'space'), may hold values from -6 to 6
- mask_one: int32 [12, 64, 16, 8192], P('dp', 'space'), may hold values 0 or 1
- place_one: int32 [12, 64, 16, 1024], P('dp', 'space'), may hold values from 0 to 7
- pooled_one: bfloat16 [12, 64, 16, 1024], P('dp', 'space'), may hold values from 0 to 2
- w_two: bfloat16 [27, 16, 32], replicated, may hold values from -0.21875 to 0.21875
- mask_two: int32 [12, 64, 32, 1024], P('dp', 'space'), may hold values 0 or 1
- place_two: int32 [12, 64, 32, 128], P('dp', 'space'), may hold values from 0 to 7
- grad_two: bfloat16 [12, 64, 32, 128], P('dp', 'space'), may hold values from -24 to 24
Outputs:
- grad_pooled: bfloat16 [12, 64, 16, 1024], P('dp', 'space')
- grad_w_one: float32 [27, 4, 16], replicated
- grad_w_two: float32 [27, 16, 32], replicated
All inputs are finite; a program needn't handle non-finite values. No bound on the sum of `mask_one` or of `mask_two` on one device may be relied on, other than what follows from the above.
Results may differ from a plain program's by a relative error of at most 0.0029.
Values may be sent and summed in bfloat16 or wider, within the bound.
A program may use at most 128 MiB of HBM per device.

v0:
```python
import jax
import jax.numpy as jnp
from jax import lax
from jax.experimental import pallas as pl
from jax.experimental.pallas import tpu as pltpu
from jax.sharding import PartitionSpec as P

C_IN, C_ONE, C_TWO = 4, 16, 32
BX, BY, BZ = 4, 8, 256
S = 3
MESH = pl.DeviceIdType.MESH
F32, BF16, I32 = jnp.float32, jnp.bfloat16, jnp.int32
TILES = 20
TOTAL = 6291456
NEIGHBOURS = [
    (di, dj, dk)
    for di in (-1, 0, 1)
    for dj in (-1, 0, 1)
    for dk in (-1, 0, 1)
    if (di, dj, dk) != (0, 0, 0)
]
XY = [(di, dj) for di in (-1, 0, 1) for dj in (-1, 0, 1) if (di, dj) != (0, 0)]
NT = (((1,), (1,)), ((), ()))
NN = (((1,), (0,)), ((), ()))
TN = (((0,), (0,)), ((), ()))


def dot(a, b, dims=NN):
    return lax.dot_general(a, b, dims, preferred_element_type=F32)


def iota(shape, dim):
    return lax.broadcasted_iota(I32, shape, dim)


def one_hot(cond):
    return jnp.where(cond, 1.0, 0.0).astype(BF16)


def kernel(
    inp, mask_one, place_one, pooled, w_two, mask_two, place_two, grad_two,
    gp_out, w1_out, w2_out,
    mp, yb, tk, rx, ry, rt, z3, wp, pst, tbuf,
    iyb, rix, riy, in32, ko, rk, lhs, sel, gc, acc1,
    wg, r1, r2, fin,
    g_send, g_recv, i_send, i_recv, k_send, k_recv,
    s1_send, s1_recv, s2_send, s2_recv, s3_send, s3_recv,
):
    dp = lax.axis_index("dp")
    sp = lax.axis_index("space")
    bi, bj, bk = sp // 16, (sp // 4) % 4, sp % 4
    zc, t8 = sp // 8, sp % 8
    men = dp * 8 + t8

    def near(di, dj, dk):
        other = ((bi + di + 4) % 4) * 16 + ((bj + dj + 4) % 4) * 4 + (bk + dk + 4) % 4
        return {"space": other}

    def plane(n):
        return {"dp": n // 8, "space": zc * 8 + n % 8}

    def column(zz):
        return {"space": zz * 8 + t8}

    barrier = pltpu.get_barrier_semaphore()
    for d in NEIGHBOURS:
        pl.semaphore_signal(barrier, inc=1, device_id=near(*d), device_id_type=MESH)
    for n in range(1, 32):
        pl.semaphore_signal(barrier, inc=1, device_id=plane((men + n) % 32), device_id_type=MESH)
    for n in range(1, 8):
        pl.semaphore_signal(barrier, inc=1, device_id=column((zc + n) % 8), device_id_type=MESH)

    er, ec = iota((128, 768), 0), iota((128, 768), 1)
    ez = ec % 128 - (ec // 256 - 1)
    e3 = one_hot((er // 64 == (ec // 128) % 2) & (ez >= 0) & (ez < 128) & (ez // 2 == er % 64))
    e0 = e3[:, 256:512]
    p_b = place_two[...].astype(F32).astype(BF16)
    p_up = dot(p_b, e0)
    par = (iota((96, 256), 1) % 2).astype(F32)
    keep = jnp.zeros((96, 256), jnp.bool_)
    for dx in range(2):
        for dy in range(2):
            tiles = [(dx * 4 + 2 * qy + dy) * 128 for qy in range(2)]
            m = jnp.concatenate([mask_two[:, t : t + 128] for t in tiles], axis=1)
            keep = keep | ((p_up == par + float(4 * dx + 2 * dy)) & (m == 1))
    kept = dot(one_hot(keep), e0, NT)
    m_f = jnp.where(kept > 0.5, grad_two[...].astype(F32), 0.0)
    p_f = p_b.astype(F32)
    m_b = m_f.astype(BF16)
    mp[0] = m_b
    mp[1] = p_b
    low = iota((96, 128), 1) < 64
    yb[0] = jnp.where(low, m_f, pltpu.roll(p_f, 64, 1)).astype(BF16)
    yb[1] = jnp.where(low, pltpu.roll(m_f, 64, 1), p_f).astype(BF16)
    tr, tc = iota((16, 128), 0), iota((16, 128), 1)
    tk[...] = jnp.zeros_like(tk)
    for side, edge in ((0, 63), (1, 0)):
        pick_m = one_hot((tr < 2) & (tc == tr * 64 + edge))
        pick_p = one_hot((tr >= 2) & (tr < 4) & (tc == (tr - 2) * 64 + edge))
        tk[side, :, 0:96] = (dot(pick_m, m_b, NT) + dot(pick_p, p_b, NT)).astype(BF16)

    for q, y in ((0, 0), (1, 7)):
        for x in range(4):
            at = x * 2048 + y * 256
            iyb[q, :, :, x * 256 : (x + 1) * 256] = inp[:, :, at : at + 256]

    pl.semaphore_wait(barrier, 64)

    def g_copy(n, d):
        di, dj, dk = d
        if dk != 0:
            src = tk.at[0 if dk > 0 else 1]
            dst = rt.at[(1 - di) * 3 + 1 - dj, 0 if dk > 0 else 1]
        elif dj == 0:
            src, dst = mp, rx.at[(1 - di) // 2]
        else:
            src = yb.at[(1 + dj) // 2]
            dst = ry.at[1 - di, (1 - dj) // 2]
        return pltpu.make_async_remote_copy(
            src_ref=src, dst_ref=dst, send_sem=g_send.at[n], recv_sem=g_recv.at[n],
            device_id=near(*d), device_id_type=MESH,
        )

    def i_copy(n, d):
        di, dj = d
        if dj == 0:
            at = 3 * 2048 if di > 0 else 0
            src, dst = inp.at[:, :, at : at + 2048], rix.at[(1 - di) // 2]
        else:
            q = (1 + dj) // 2
            if di == 0:
                src = iyb.at[q]
                dst = riy.at[(1 - dj) // 2, :, :, 256 : 256 + 1024]
            else:
                at = 768 if di > 0 else 0
                to = 0 if di > 0 else 1280
                src = iyb.at[q, :, :, at : at + 256]
                dst = riy.at[(1 - dj) // 2, :, :, to : to + 256]
        return pltpu.make_async_remote_copy(
            src_ref=src, dst_ref=dst, send_sem=i_send.at[n], recv_sem=i_recv.at[n],
            device_id=near(di, dj, 0), device_id_type=MESH,
        )

    g_copies = [g_copy(n, d) for n, d in enumerate(NEIGHBOURS)]
    i_copies = [i_copy(n, d) for n, d in enumerate(XY)]
    for d, c in zip(NEIGHBOURS, g_copies):
        if d[2] != 0:
            c.start()
    for d, c in zip(NEIGHBOURS, g_copies):
        if d[2] == 0:
            c.start()
    for c in i_copies:
        c.start()

    for o9 in range(9):
        wp[o9 * 16 : o9 * 16 + 16, :] = jnp.concatenate(
            [w_two[o9 * 3 + b].astype(F32) for b in range(3)], axis=1
        ).astype(BF16)
    pst[...] = jnp.zeros_like(pst)
    for ox in range(3):
        for oy in range(3):
            o9 = ox * 3 + oy
            for qx in range(2):
                for qy in range(4):
                    to = ((qx + 2 - ox) * 6 + qy + 2 - oy) * 128
                    at = (qx * 4 + qy) * 128
                    for s in range(S):
                        pst[s, o9 * 16 : o9 * 16 + 16, to : to + 128] = pooled[
                            s * 16 : s * 16 + 16, at : at + 128
                        ]
    e1r, e1c = iota((128, 256), 0), iota((128, 256), 1)
    e1 = one_hot(e1c // 2 == e1r)
    par1 = (iota((48, 256), 1) % 2).astype(F32)
    for hx in range(2):
        for hy in range(4):
            at = (hx * 4 + hy) * 128
            up = dot(place_one[:, at : at + 128].astype(F32).astype(BF16), e1)
            for dx in range(2):
                for dy in range(2):
                    to = ((2 * hx + dx) * 8 + 2 * hy + dy) * 256
                    ok = (up == par1 + float(4 * dx + 2 * dy)) & (mask_one[:, to : to + 256] == 1)
                    sel[:, to : to + 256] = one_hot(ok)

    for n in range(8):
        i_copies[n].wait_recv()
    in32[...] = jnp.zeros_like(in32)
    for s in range(S):
        for x in range(6):
            for y in range(10):
                if 1 <= y <= 8:
                    if 1 <= x <= 4:
                        at = ((x - 1) * 8 + y - 1) * 256
                        v = inp[s, :, at : at + 256]
                    else:
                        at = (y - 1) * 256
                        v = rix[0 if x == 0 else 1, s, :, at : at + 256]
                else:
                    v = riy[0 if y == 0 else 1, s, :, x * 256 : x * 256 + 256]
                in32[s * 6 + x, 4 * y : 4 * y + 4, :] = v.astype(F32)
    lane48 = iota((48, 128), 1)
    for side in range(2):
        o = jnp.zeros((48, 128), F32)
        for l in range(18):
            tile = in32[l, :, 128:256] if side == 0 else in32[l, :, 0:128]
            edge = 127 if side == 0 else 0
            o = jnp.where(lane48 == l, pltpu.roll(tile, (l - edge) % 128, 1), o)
        ko[side] = o

    def k_copy(side):
        return pltpu.make_async_remote_copy(
            src_ref=ko.at[side], dst_ref=rk.at[side],
            send_sem=k_send.at[side], recv_sem=k_recv.at[side],
            device_id=near(0, 0, 1 if side == 0 else -1), device_id_type=MESH,
        )

    k_copies = [k_copy(0), k_copy(1)]
    for c in k_copies:
        c.start()

    for n in range(26):
        g_copies[n].wait_recv()
    fr, fc = iota((32, 768), 0), iota((32, 768), 1)
    f_in, f_mid, f_b = fc % 128, (fc // 128) % 2, fc // 256
    left = (f_b == 2) & (f_in == 0)
    right = (f_b == 0) & (f_in == 127)

    def halo_rows(row):
        return one_hot((left & (fr == row)) | (right & (fr == 16 + row)))

    f_m, f_p = halo_rows(f_mid), halo_rows(2 + f_mid)
    f_y = [halo_rows(2 * f_mid + q) for q in range(2)]
    lane = (iota((96, 128), 1) % 2).astype(F32)
    dz = [1.0 - lane, lane, 1.0 - lane]

    def put(b, x, y, dx, dy, um, up):
        v = jnp.where(up == dz[b] + float(4 * dx + 2 * dy), um, 0.0).astype(BF16)
        to = (x * 6 + y) * 128
        for s in range(S):
            z3[s, b * 32 : b * 32 + 32, to : to + 128] = v[s * 32 : s * 32 + 32]

    for di in (-1, 0, 1):
        for dj in (-1, 0, 1):
            stack = rt[(di + 1) * 3 + dj + 1].reshape(32, 128)[:, 0:96]
            xs = {-1: [(0, 1)], 0: [(1, 0), (2, 1)], 1: [(3, 0)]}[di]
            if dj == 0:
                ref = mp if di == 0 else rx.at[(di + 1) // 2]
                um = dot(ref[0], e3) + dot(stack, f_m, TN)
                up = dot(ref[1], e3) + dot(stack, f_p, TN)
                for b in range(3):
                    for qy in range(2):
                        at = (b * 2 + qy) * 128
                        for x, dx in xs:
                            for dy in range(2):
                                put(b, x, 1 + 2 * qy + dy, dx, dy, um[:, at : at + 128], up[:, at : at + 128])
            else:
                q = 1 if dj < 0 else 0
                u = dot(ry[di + 1, (dj + 1) // 2], e3) + dot(stack, f_y[q], TN)
                for b in range(3):
                    at = b * 256
                    for x, dx in xs:
                        put(b, x, 0 if dj < 0 else 5, dx, q, u[:, at : at + 128], u[:, at + 128 : at + 256])

    w2 = jnp.zeros((144, 96), F32)
    for s in range(S):
        for x in range(4):
            tbuf[:, x * 768 : x * 768 + 768] = dot(wp[...], z3[s, :, x * 768 : x * 768 + 768])
        w2 = w2 + dot(pst[s], z3[s], NT)
        for x in range(2):
            for y in range(4):
                a = jnp.zeros((16, 128), F32)
                for ox in range(3):
                    for oy in range(3):
                        r = (ox * 3 + oy) * 16
                        at = ((x + 2 - ox) * 6 + y + 2 - oy) * 128
                        a = a + tbuf[r : r + 16, at : at + 128]
                gp_out[s * 16 : s * 16 + 16, (x * 4 + y) * 128 : (x * 4 + y) * 128 + 128] = a.astype(BF16)
    w2 = jnp.concatenate([w2, jnp.zeros((144, 32), F32)], axis=1)
    for i in range(18):
        wg[i] = w2[i * 8 : i * 8 + 8]

    for c in k_copies:
        c.wait_recv()
    lane256 = iota((48, 256), 1)
    for l in range(18):
        v = in32[l]
        below = jnp.concatenate([pltpu.roll(rk[0], (0 - l) % 128, 1), jnp.zeros((48, 128), F32)], axis=1)
        above = jnp.concatenate([jnp.zeros((48, 128), F32), pltpu.roll(rk[1], (127 - l) % 128, 1)], axis=1)
        lhs[l, 0:48, :] = jnp.where(lane256 == 0, below, pltpu.roll(v, 1, 1)).astype(BF16)
        lhs[l, 48:96, :] = v.astype(BF16)
        lhs[l, 96:144, :] = jnp.where(lane256 == 255, above, pltpu.roll(v, 255, 1)).astype(BF16)

    for hx in range(2):
        for hy in range(4):
            at = (hx * 4 + hy) * 128
            up = dot(gp_out[:, at : at + 128], e1)
            for dx in range(2):
                for dy in range(2):
                    x, y = 2 * hx + dx, 2 * hy + dy
                    to = (x * 8 + y) * 256
                    v = (up * sel[:, to : to + 256].astype(F32)).astype(BF16)
                    for s in range(S):
                        gc[s, x, y * 16 : y * 16 + 16, :] = v[s * 16 : s * 16 + 16]
    a1 = jnp.zeros((432, 128), F32)
    for s in range(S):
        for x in range(4):
            three = lhs[s * 6 + x : s * 6 + x + 3].reshape(432, 256)
            a1 = a1 + dot(three, gc[s, x], NT)
    acc1[...] = a1

    row8, lane8 = iota((8, 128), 0), iota((8, 128), 1)
    packed = [jnp.zeros((8, 128), F32), jnp.zeros((8, 128), F32)]
    for ox in range(3):
        for oy in range(3):
            for b in range(3):
                o = ox * 9 + oy * 3 + b
                t = jnp.zeros((8, 128), F32)
                for i in range(5):
                    r = ox * 144 + b * 48 + i * 8
                    t = t + jnp.where(2 * i + row8 // 4 == lane8 // 16 + oy, acc1[r : r + 8, :], 0.0)
                t = t + pltpu.roll(t, 4, 0)
                t = t + pltpu.roll(t, 16, 1)
                t = t + pltpu.roll(t, 32, 1)
                t = t + pltpu.roll(t, 64, 1)
                k = o % 16
                packed[o // 16] = jnp.where(
                    (row8 // 4 == k // 8) & (lane8 // 16 == k % 8), t, packed[o // 16]
                )
    wg[18] = packed[0]
    wg[19] = packed[1]

    def p1(o):
        return pltpu.make_async_remote_copy(
            src_ref=wg.at[o], dst_ref=r1.at[men], send_sem=s1_send.at[o], recv_sem=s1_recv.at[men],
            device_id=plane(o), device_id_type=MESH,
        )

    def p1_from(n):
        return pltpu.make_async_remote_copy(
            src_ref=wg.at[0], dst_ref=r1.at[n], send_sem=s1_send.at[0], recv_sem=s1_recv.at[n],
            device_id=plane(n), device_id_type=MESH,
        )

    def p2(zz):
        return pltpu.make_async_remote_copy(
            src_ref=r2.at[zc], dst_ref=r2.at[zc], send_sem=s2_send.at[zz], recv_sem=s2_recv.at[zc],
            device_id=column(zz), device_id_type=MESH,
        )

    def p2_from(zz):
        return pltpu.make_async_remote_copy(
            src_ref=r2.at[zz], dst_ref=r2.at[zz], send_sem=s2_send.at[zz], recv_sem=s2_recv.at[zz],
            device_id=column(zz), device_id_type=MESH,
        )

    def p3(n):
        return pltpu.make_async_remote_copy(
            src_ref=fin.at[men], dst_ref=fin.at[men], send_sem=s3_send.at[n], recv_sem=s3_recv.at[men],
            device_id=plane(n), device_id_type=MESH,
        )

    def p3_from(o):
        return pltpu.make_async_remote_copy(
            src_ref=fin.at[o], dst_ref=fin.at[o], send_sem=s3_send.at[0], recv_sem=s3_recv.at[o],
            device_id=plane(o), device_id_type=MESH,
        )

    for o in range(TILES):
        @pl.when(men != o)
        def _():
            p1(o).start()

    owner = men < TILES

    @pl.when(owner)
    def _():
        r1[men] = wg[men]
        for n in range(32):
            @pl.when(men != n)
            def _():
                p1_from(n).wait_recv()
        total = r1[0]
        for n in range(1, 32):
            total = total + r1[n]
        r2[zc] = total
        for zz in range(8):
            @pl.when(zc != zz)
            def _():
                p2(zz).start()
        for zz in range(8):
            @pl.when(zc != zz)
            def _():
                p2_from(zz).wait_recv()
        total = r2[0]
        for zz in range(1, 8):
            total = total + r2[zz]
        fin[men] = total
        for n in range(32):
            @pl.when(men != n)
            def _():
                p3(n).start()

    for o in range(TILES):
        @pl.when(men != o)
        def _():
            p3_from(o).wait_recv()

    for o9 in range(9):
        for h in range(2):
            v = fin[2 * o9 + h] * (float(TOTAL // 8) ** -0.5)
            for b in range(3):
                w2_out[o9 * 3 + b, h * 8 : h * 8 + 8, :] = v[:, b * 32 : b * 32 + 32]
    for i in range(2):
        v = fin[18 + i] * (float(TOTAL) ** -0.5)
        for k in range(16 if i == 0 else 11):
            w1_out[i * 16 + k] = v[(k // 8) * 4 : (k // 8) * 4 + 4, (k % 8) * 16 : (k % 8) * 16 + 16]

    for c in g_copies + i_copies + k_copies:
        c.wait_send()
    for o in range(TILES):
        @pl.when(men != o)
        def _():
            p1(o).wait_send()

    @pl.when(owner)
    def _():
        for zz in range(8):
            @pl.when(zc != zz)
            def _():
                p2(zz).wait_send()
        for n in range(32):
            @pl.when(men != n)
            def _():
                p3(n).wait_send()


def local(inputs, mask_one, place_one, pooled_one, w_two, mask_two, place_two, grad_two):
    vm = pl.BlockSpec(memory_space=pltpu.VMEM)
    dma = pltpu.SemaphoreType.DMA
    gp, w1, w2 = pl.pallas_call(
        kernel,
        out_shape=(
            jax.ShapeDtypeStruct((48, 1024), BF16),
            jax.ShapeDtypeStruct((27, 4, 16), F32),
            jax.ShapeDtypeStruct((27, 16, 32), F32),
        ),
        in_specs=[vm] * 8,
        out_specs=(vm, vm, vm),
        scratch_shapes=[
            pltpu.VMEM((2, 96, 128), BF16),
            pltpu.VMEM((2, 96, 128), BF16),
            pltpu.VMEM((2, 16, 128), BF16),
            pltpu.VMEM((2, 2, 96, 128), BF16),
            pltpu.VMEM((3, 2, 96, 128), BF16),
            pltpu.VMEM((9, 2, 16, 128), BF16),
            pltpu.VMEM((S, 96, 3072), BF16),
            pltpu.VMEM((144, 96), BF16),
            pltpu.VMEM((S, 144, 3072), BF16),
            pltpu.VMEM((144, 3072), F32),
            pltpu.VMEM((2, S, 4, 1024), BF16),
            pltpu.VMEM((2, S, 4, 2048), BF16),
            pltpu.VMEM((2, S, 4, 1536), BF16),
            pltpu.VMEM((18, 48, 256), F32),
            pltpu.VMEM((2, 48, 128), F32),
            pltpu.VMEM((2, 48, 128), F32),
            pltpu.VMEM((18, 144, 256), BF16),
            pltpu.VMEM((48, 8192), BF16),
            pltpu.VMEM((S, 4, 128, 256), BF16),
            pltpu.VMEM((432, 128), F32),
            pltpu.VMEM((TILES, 8, 128), F32),
            pltpu.VMEM((32, 8, 128), F32),
            pltpu.VMEM((8, 8, 128), F32),
            pltpu.VMEM((TILES, 8, 128), F32),
            dma((26,)), dma((26,)), dma((8,)), dma((8,)), dma((2,)), dma((2,)),
            dma((TILES,)), dma((32,)), dma((8,)), dma((8,)), dma((32,)), dma((TILES,)),
        ],
        compiler_params=pltpu.CompilerParams(
            collective_id=0, has_side_effects=True, vmem_limit_bytes=56 * 1024 * 1024
        ),
        name="whole",
    )(
        inputs.reshape(S, 4, 8192),
        mask_one.reshape(48, 8192),
        place_one.reshape(48, 1024),
        pooled_one.reshape(48, 1024),
        w_two,
        mask_two.reshape(96, 1024),
        place_two.reshape(96, 128),
        grad_two.reshape(96, 128),
    )
    return gp.reshape(S, 1, 16, 1024), w1, w2


def solution(mesh):
    spec = P("dp", "space", None, None)
    return jax.shard_map(
        local,
        mesh=mesh,
        in_specs=(spec, spec, spec, spec, P(), spec, spec, spec),
        out_specs=(spec, P(), P()),
        check_vma=False,
    )
```

profile of v0, /device:TPU:1, one launch (start us, length us, event | category | flops | bytes accessed | tf_op | source)
XLA Modules:
  0.0 53.8 jit_solution(16290271801011700609)
XLA Ops:
  0.6 48.4 %whole.1 = (bf16[48,1024]{1,0:T(8,128)(2,1)}, f32[27,4,16]{2,1,0:T(4,128)}, f32[27,16,32]{2,1,0:T(8,128)}) custom-call(bf16[3,4,8192]{2,1,0:T(4,128)(2,1)} %bitcast.12, s32[48,8192]{1,0:T(8,128)} %bitcast.10, s32[48,1024]{1,0:T(8,128)} %bitcast.13, bf16[48,1024]{1,0:T(8,128)(2,1)} %bitcast.14, bf16[27,16,32]{2,1,0:T(8,128)(2,1)} %w_two.1, ...), custom_call_target="tpu_custom_call" | custom-call | tf_op jit(solution)/shard_map/whole/pallas_call | solution.py:439
  49.1 1.5 %copy.12 = f32[27,4,16]{0,2,1:T(8,128)} copy(f32[27,4,16]{2,1,0:T(4,128)} %get-tuple-element.10) | data formatting | bytes 13824
  50.6 1.5 %copy.15 = bf16[3,1,16,1024]{3,2,1,0:T(8,128)(2,1)} copy(bf16[3,1,16,1024]{3,2,1,0:T(8,128)(2,1)} %bitcast.15) | data formatting | bytes 196608
  52.1 1.6 %copy.16 = f32[27,16,32]{2,1,0:T(8,128)} copy(f32[27,16,32]{2,1,0:T(8,128)} %get-tuple-element.17) | data formatting | bytes 110592
where the time goes:
time: 54 us; the launch traced here: 53.8 us
  Pallas kernels  48.4 us (90%)
  local copies, waits for them, and re-layouts  4.69 us (9%)
  between operations  0.64 us (1%)
    pallas_call x1, Pallas kernels, local(): pl.pallas_call(kernel, out_shape=(jax.ShapeDtypeStruct((48, 1024), BF16),...  48.4 us
    unnamed x3, local copies, waits for them, and re-layouts  4.69 us

commit v1 on v0

--- a/solution.py
+++ b/solution.py
@@ -10,7 +10,7 @@
 S = 3
 MESH = pl.DeviceIdType.MESH
 F32, BF16, I32 = jnp.float32, jnp.bfloat16, jnp.int32
-TILES = 20
+TILES = 18
 TOTAL = 6291456
 NEIGHBOURS = [
     (di, dj, dk)
@@ -38,13 +38,16 @@
 
 
 def kernel(
-    inp, mask_one, place_one, pooled, w_two, mask_two, place_two, grad_two,
-    gp_out, w1_out, w2_out,
+    inp_h, mask_one_h, place_one_h, pooled_h, w_two_h, mask_two_h, place_two_h, grad_two_h,
+    gp_h, fin_h,
+    inp, mask_one, place_one, pooled, w_two, mask_two, place_two, grad_two, gp,
     mp, yb, tk, rx, ry, rt, z3, wp, pst, tbuf,
     iyb, rix, riy, in32, ko, rk, lhs, sel, gc, acc1,
-    wg, r1, r2, fin,
+    wg, r1, r2, fin, qbuf, own1, c1, c2, c3,
     g_send, g_recv, i_send, i_recv, k_send, k_recv,
     s1_send, s1_recv, s2_send, s2_recv, s3_send, s3_recv,
+    t1_send, t1_recv, t2_send, t2_recv, t3_send, t3_recv, t4_send, t4_recv,
+    l_sem, o_sem,
 ):
     dp = lax.axis_index("dp")
     sp = lax.axis_index("space")
@@ -61,6 +64,93 @@
 
     def column(zz):
         return {"space": zz * 8 + t8}
+
+    def p1(o):
+        return pltpu.make_async_remote_copy(
+            src_ref=wg.at[o], dst_ref=r1.at[men], send_sem=s1_send.at[o], recv_sem=s1_recv.at[men],
+            device_id=plane(o), device_id_type=MESH,
+        )
+
+    def p1_from(n):
+        return pltpu.make_async_remote_copy(
+            src_ref=wg.at[0], dst_ref=r1.at[n], send_sem=s1_send.at[0], recv_sem=s1_recv.at[n],
+            device_id=plane(n), device_id_type=MESH,
+        )
+
+    def p2(zz):
+        return pltpu.make_async_remote_copy(
+            src_ref=r2.at[zc], dst_ref=r2.at[zc], send_sem=s2_send.at[zz], recv_sem=s2_recv.at[zc],
+            device_id=column(zz), device_id_type=MESH,
+        )
+
+    def p2_from(zz):
+        return pltpu.make_async_remote_copy(
+            src_ref=r2.at[zz], dst_ref=r2.at[zz], send_sem=s2_send.at[zz], recv_sem=s2_recv.at[zz],
+            device_id=column(zz), device_id_type=MESH,
+        )
+
+    def p3(n):
+        return pltpu.make_async_remote_copy(
+            src_ref=fin.at[men], dst_ref=fin.at[men], send_sem=s3_send.at[n], recv_sem=s3_recv.at[men],
+            device_id=plane(n), device_id_type=MESH,
+        )
+
+    def p3_from(o):
+        return pltpu.make_async_remote_copy(
+            src_ref=fin.at[o], dst_ref=fin.at[o], send_sem=s3_send.at[0], recv_sem=s3_recv.at[o],
+            device_id=plane(o), device_id_type=MESH,
+        )
+
+    core = dp % 2
+    chip = (dp // 2) * 8 + t8
+
+    def twin():
+        return {"dp": dp + 1 - 2 * core}
+
+    def chip_at(n):
+        return {"dp": (n // 8) * 2 + core, "space": zc * 8 + n % 8}
+
+    def t1():
+        return pltpu.make_async_remote_copy(
+            src_ref=own1.at[1 - core], dst_ref=c1, send_sem=t1_send, recv_sem=t1_recv,
+            device_id=twin(), device_id_type=MESH,
+        )
+
+    def t2(n, slot):
+        return pltpu.make_async_remote_copy(
+            src_ref=c2.at[slot], dst_ref=c2.at[slot], send_sem=t2_send.at[n], recv_sem=t2_recv.at[slot],
+            device_id=chip_at(n), device_id_type=MESH,
+        )
+
+    def t3(n, slot):
+        return pltpu.make_async_remote_copy(
+            src_ref=c3.at[slot], dst_ref=c3.at[slot], send_sem=t3_send.at[n], recv_sem=t3_recv.at[slot],
+            device_id=column(n), device_id_type=MESH,
+        )
+
+    def t4(slot):
+        return pltpu.make_async_remote_copy(
+            src_ref=fin.at[TILES + slot], dst_ref=fin.at[TILES + slot], send_sem=t4_send, recv_sem=t4_recv,
+            device_id=twin(), device_id_type=MESH,
+        )
+
+    loads = [
+        pltpu.make_async_copy(a, b, l_sem.at[n])
+        for n, (a, b) in enumerate(
+            (
+                (place_two_h, place_two),
+                (mask_two_h, mask_two),
+                (grad_two_h, grad_two),
+                (inp_h, inp),
+                (w_two_h, w_two),
+                (pooled_h, pooled),
+                (place_one_h, place_one),
+                (mask_one_h, mask_one),
+            )
+        )
+    ]
+    for c in loads:
+        c.start()
 
     barrier = pltpu.get_barrier_semaphore()
     for d in NEIGHBOURS:
@@ -74,6 +164,8 @@
     ez = ec % 128 - (ec // 256 - 1)
     e3 = one_hot((er // 64 == (ec // 128) % 2) & (ez >= 0) & (ez < 128) & (ez // 2 == er % 64))
     e0 = e3[:, 256:512]
+    for c in loads[:3]:
+        c.wait()
     p_b = place_two[...].astype(F32).astype(BF16)
     p_up = dot(p_b, e0)
     par = (iota((96, 256), 1) % 2).astype(F32)
@@ -99,6 +191,7 @@
         pick_p = one_hot((tr >= 2) & (tr < 4) & (tc == (tr - 2) * 64 + edge))
         tk[side, :, 0:96] = (dot(pick_m, m_b, NT) + dot(pick_p, p_b, NT)).astype(BF16)
 
+    loads[3].wait()
     for q, y in ((0, 0), (1, 7)):
         for x in range(4):
             at = x * 2048 + y * 256
@@ -152,6 +245,12 @@
     for c in i_copies:
         c.start()
 
+    qr, qc = iota((432, 128), 0), iota((432, 128), 1)
+    for oy in range(3):
+        qo = (qr // 144) * 9 + oy * 3 + (qr // 48) % 3
+        qbuf[oy] = one_hot((qr % 4 == qc // 32) & (qc % 32 == qo) & (qr % 48 < 40))
+    for c in loads[4:]:
+        c.wait()
     for o9 in range(9):
         wp[o9 * 16 : o9 * 16 + 16, :] = jnp.concatenate(
             [w_two[o9 * 3 + b].astype(F32) for b in range(3)], axis=1
@@ -181,6 +280,75 @@
                     ok = (up == par1 + float(4 * dx + 2 * dy)) & (mask_one[:, to : to + 256] == 1)
                     sel[:, to : to + 256] = one_hot(ok)
 
+    for n in range(26):
+        g_copies[n].wait_recv()
+    fr, fc = iota((32, 768), 0), iota((32, 768), 1)
+    f_in, f_mid, f_b = fc % 128, (fc // 128) % 2, fc // 256
+    left = (f_b == 2) & (f_in == 0)
+    right = (f_b == 0) & (f_in == 127)
+
+    def halo_rows(row):
+        return one_hot((left & (fr == row)) | (right & (fr == 16 + row)))
+
+    f_m, f_p = halo_rows(f_mid), halo_rows(2 + f_mid)
+    f_y = [halo_rows(2 * f_mid + q) for q in range(2)]
+    lane = (iota((96, 128), 1) % 2).astype(F32)
+    dz = [1.0 - lane, lane, 1.0 - lane]
+
+    def put(b, x, y, dx, dy, um, up):
+        v = jnp.where(up == dz[b] + float(4 * dx + 2 * dy), um, 0.0).astype(BF16)
+        to = (x * 6 + y) * 128
+        for s in range(S):
+            z3[s, b * 32 : b * 32 + 32, to : to + 128] = v[s * 32 : s * 32 + 32]
+
+    for di in (-1, 0, 1):
+        for dj in (-1, 0, 1):
+            stack = rt[(di + 1) * 3 + dj + 1].reshape(32, 128)[:, 0:96]
+            xs = {-1: [(0, 1)], 0: [(1, 0), (2, 1)], 1: [(3, 0)]}[di]
+            if dj == 0:
+                ref = mp if di == 0 else rx.at[(di + 1) // 2]
+                um = dot(ref[0], e3) + dot(stack, f_m, TN)
+                up = dot(ref[1], e3) + dot(stack, f_p, TN)
+                for b in range(3):
+                    for qy in range(2):
+                        at = (b * 2 + qy) * 128
+                        for x, dx in xs:
+                            for dy in range(2):
+                                put(b, x, 1 + 2 * qy + dy, dx, dy, um[:, at : at + 128], up[:, at : at + 128])
+            else:
+                q = 1 if dj < 0 else 0
+                u = dot(ry[di + 1, (dj + 1) // 2], e3) + dot(stack, f_y[q], TN)
+                for b in range(3):
+                    at = b * 256
+                    for x, dx in xs:
+                        put(b, x, 0 if dj < 0 else 5, dx, q, u[:, at : at + 128], u[:, at + 128 : at + 256])
+
+    w2 = jnp.zeros((144, 96), F32)
+    for s in range(S):
+        w2 = w2 + dot(pst[s], z3[s], NT)
+    w2 = jnp.concatenate([w2, jnp.zeros((144, 32), F32)], axis=1)
+    for i in range(TILES):
+        wg[i] = w2[i * 8 : i * 8 + 8]
+    for o in range(TILES):
+        @pl.when(men != o)
+        def _():
+            p1(o).start()
+
+    for s in range(S):
+        for x in range(4):
+            tbuf[:, x * 768 : x * 768 + 768] = dot(wp[...], z3[s, :, x * 768 : x * 768 + 768])
+        for x in range(2):
+            for y in range(4):
+                a = jnp.zeros((16, 128), F32)
+                for ox in range(3):
+                    for oy in range(3):
+                        r = (ox * 3 + oy) * 16
+                        at = ((x + 2 - ox) * 6 + y + 2 - oy) * 128
+                        a = a + tbuf[r : r + 16, at : at + 128]
+                gp[s * 16 : s * 16 + 16, (x * 4 + y) * 128 : (x * 4 + y) * 128 + 128] = a.astype(BF16)
+    gp_copy = pltpu.make_async_copy(gp, gp_h, o_sem.at[0])
+    gp_copy.start()
+
     for n in range(8):
         i_copies[n].wait_recv()
     in32[...] = jnp.zeros_like(in32)
@@ -217,67 +385,6 @@
     for c in k_copies:
         c.start()
 
-    for n in range(26):
-        g_copies[n].wait_recv()
-    fr, fc = iota((32, 768), 0), iota((32, 768), 1)
-    f_in, f_mid, f_b = fc % 128, (fc // 128) % 2, fc // 256
-    left = (f_b == 2) & (f_in == 0)
-    right = (f_b == 0) & (f_in == 127)
-
-    def halo_rows(row):
-        return one_hot((left & (fr == row)) | (right & (fr == 16 + row)))
-
-    f_m, f_p = halo_rows(f_mid), halo_rows(2 + f_mid)
-    f_y = [halo_rows(2 * f_mid + q) for q in range(2)]
-    lane = (iota((96, 128), 1) % 2).astype(F32)
-    dz = [1.0 - lane, lane, 1.0 - lane]
-
-    def put(b, x, y, dx, dy, um, up):
-        v = jnp.where(up == dz[b] + float(4 * dx + 2 * dy), um, 0.0).astype(BF16)
-        to = (x * 6 + y) * 128
-        for s in range(S):
-            z3[s, b * 32 : b * 32 + 32, to : to + 128] = v[s * 32 : s * 32 + 32]
-
-    for di in (-1, 0, 1):
-        for dj in (-1, 0, 1):
-            stack = rt[(di + 1) * 3 + dj + 1].reshape(32, 128)[:, 0:96]
-            xs = {-1: [(0, 1)], 0: [(1, 0), (2, 1)], 1: [(3, 0)]}[di]
-            if dj == 0:
-                ref = mp if di == 0 else rx.at[(di + 1) // 2]
-                um = dot(ref[0], e3) + dot(stack, f_m, TN)
-                up = dot(ref[1], e3) + dot(stack, f_p, TN)
-                for b in range(3):
-                    for qy in range(2):
-                        at = (b * 2 + qy) * 128
-                        for x, dx in xs:
-                            for dy in range(2):
-                                put(b, x, 1 + 2 * qy + dy, dx, dy, um[:, at : at + 128], up[:, at : at + 128])
-            else:
-                q = 1 if dj < 0 else 0
-                u = dot(ry[di + 1, (dj + 1) // 2], e3) + dot(stack, f_y[q], TN)
-                for b in range(3):
-                    at = b * 256
-                    for x, dx in xs:
-                        put(b, x, 0 if dj < 0 else 5, dx, q, u[:, at : at + 128], u[:, at + 128 : at + 256])
-
-    w2 = jnp.zeros((144, 96), F32)
-    for s in range(S):
-        for x in range(4):
-            tbuf[:, x * 768 : x * 768 + 768] = dot(wp[...], z3[s, :, x * 768 : x * 768 + 768])
-        w2 = w2 + dot(pst[s], z3[s], NT)
-        for x in range(2):
-            for y in range(4):
-                a = jnp.zeros((16, 128), F32)
-                for ox in range(3):
-                    for oy in range(3):
-                        r = (ox * 3 + oy) * 16
-                        at = ((x + 2 - ox) * 6 + y + 2 - oy) * 128
-                        a = a + tbuf[r : r + 16, at : at + 128]
-                gp_out[s * 16 : s * 16 + 16, (x * 4 + y) * 128 : (x * 4 + y) * 128 + 128] = a.astype(BF16)
-    w2 = jnp.concatenate([w2, jnp.zeros((144, 32), F32)], axis=1)
-    for i in range(18):
-        wg[i] = w2[i * 8 : i * 8 + 8]
-
     for c in k_copies:
         c.wait_recv()
     lane256 = iota((48, 256), 1)
@@ -292,7 +399,7 @@
     for hx in range(2):
         for hy in range(4):
             at = (hx * 4 + hy) * 128
-            up = dot(gp_out[:, at : at + 128], e1)
+            up = dot(gp[:, at : at + 128], e1)
             for dx in range(2):
                 for dy in range(2):
                     x, y = 2 * hx + dx, 2 * hy + dy
@@ -300,75 +407,32 @@
                     v = (up * sel[:, to : to + 256].astype(F32)).astype(BF16)
                     for s in range(S):
                         gc[s, x, y * 16 : y * 16 + 16, :] = v[s * 16 : s * 16 + 16]
-    a1 = jnp.zeros((432, 128), F32)
+    a1 = jnp.zeros((128, 432), F32)
     for s in range(S):
         for x in range(4):
             three = lhs[s * 6 + x : s * 6 + x + 3].reshape(432, 256)
-            a1 = a1 + dot(three, gc[s, x], NT)
+            a1 = a1 + dot(gc[s, x], three, NT)
     acc1[...] = a1
-
-    row8, lane8 = iota((8, 128), 0), iota((8, 128), 1)
-    packed = [jnp.zeros((8, 128), F32), jnp.zeros((8, 128), F32)]
-    for ox in range(3):
-        for oy in range(3):
-            for b in range(3):
-                o = ox * 9 + oy * 3 + b
-                t = jnp.zeros((8, 128), F32)
-                for i in range(5):
-                    r = ox * 144 + b * 48 + i * 8
-                    t = t + jnp.where(2 * i + row8 // 4 == lane8 // 16 + oy, acc1[r : r + 8, :], 0.0)
-                t = t + pltpu.roll(t, 4, 0)
-                t = t + pltpu.roll(t, 16, 1)
-                t = t + pltpu.roll(t, 32, 1)
-                t = t + pltpu.roll(t, 64, 1)
-                k = o % 16
-                packed[o // 16] = jnp.where(
-                    (row8 // 4 == k // 8) & (lane8 // 16 == k % 8), t, packed[o // 16]
-                )
-    wg[18] = packed[0]
-    wg[19] = packed[1]
-
-    def p1(o):
-        return pltpu.make_async_remote_copy(
-            src_ref=wg.at[o], dst_ref=r1.at[men], send_sem=s1_send.at[o], recv_sem=s1_recv.at[men],
-            device_id=plane(o), device_id_type=MESH,
-        )
-
-    def p1_from(n):
-        return pltpu.make_async_remote_copy(
-            src_ref=wg.at[0], dst_ref=r1.at[n], send_sem=s1_send.at[0], recv_sem=s1_recv.at[n],
-            device_id=plane(n), device_id_type=MESH,
-        )
-
-    def p2(zz):
-        return pltpu.make_async_remote_copy(
-            src_ref=r2.at[zc], dst_ref=r2.at[zc], send_sem=s2_send.at[zz], recv_sem=s2_recv.at[zc],
-            device_id=column(zz), device_id_type=MESH,
-        )
-
-    def p2_from(zz):
-        return pltpu.make_async_remote_copy(
-            src_ref=r2.at[zz], dst_ref=r2.at[zz], send_sem=s2_send.at[zz], recv_sem=s2_recv.at[zz],
-            device_id=column(zz), device_id_type=MESH,
-        )
-
-    def p3(n):
-        return pltpu.make_async_remote_copy(
-            src_ref=fin.at[men], dst_ref=fin.at[men], send_sem=s3_send.at[n], recv_sem=s3_recv.at[men],
-            device_id=plane(n), device_id_type=MESH,
-        )
-
-    def p3_from(o):
-        return pltpu.make_async_remote_copy(
-            src_ref=fin.at[o], dst_ref=fin.at[o], send_sem=s3_send.at[0], recv_sem=s3_recv.at[o],
-            device_id=plane(o), device_id_type=MESH,
-        )
-
-    for o in range(TILES):
-        @pl.when(men != o)
-        def _():
-            p1(o).start()
-
+    y_lane = (iota((16, 432), 1) % 48) // 4
+    parts = []
+    for oy in range(3):
+        t = jnp.zeros((16, 432), F32)
+        for y in range(8):
+            t = t + jnp.where(y_lane == y + oy, acc1[y * 16 : y * 16 + 16, :], 0.0)
+        parts.append(t)
+    w1 = jnp.zeros((16, 128), F32)
+    for oy in range(3):
+        t = parts[oy]
+        hi = t.astype(BF16)
+        t = t - hi.astype(F32)
+        mid = t.astype(BF16)
+        low_part = (t - mid.astype(F32)).astype(BF16)
+        r = dot(jnp.concatenate([hi, mid, low_part], axis=0), qbuf[oy])
+        w1 = w1 + (r[0:16] + r[16:32] + r[32:48])
+    own1[0] = w1[0:8]
+    own1[1] = w1[8:16]
+
+    t1().start()
     owner = men < TILES
 
     @pl.when(owner)
@@ -386,6 +450,16 @@
             @pl.when(zc != zz)
             def _():
                 p2(zz).start()
+
+    t1().wait_recv()
+    c2[chip] = own1[core] + c1[...]
+    for n in range(16):
+        @pl.when(chip != n)
+        def _():
+            t2(n, chip).start()
+
+    @pl.when(owner)
+    def _():
         for zz in range(8):
             @pl.when(zc != zz)
             def _():
@@ -399,20 +473,35 @@
             def _():
                 p3(n).start()
 
+    for n in range(16):
+        @pl.when(chip != n)
+        def _():
+            t2(n, n).wait_recv()
+    total = c2[0]
+    for n in range(1, 16):
+        total = total + c2[n]
+    c3[zc] = total
+    for n in range(8):
+        @pl.when(zc != n)
+        def _():
+            t3(n, zc).start()
+    for n in range(8):
+        @pl.when(zc != n)
+        def _():
+            t3(n, n).wait_recv()
+    total = c3[0]
+    for n in range(1, 8):
+        total = total + c3[n]
+    fin[TILES + core] = total
+    t4(core).start()
+
     for o in range(TILES):
         @pl.when(men != o)
         def _():
             p3_from(o).wait_recv()
-
-    for o9 in range(9):
-        for h in range(2):
-            v = fin[2 * o9 + h] * (float(TOTAL // 8) ** -0.5)
-            for b in range(3):
-                w2_out[o9 * 3 + b, h * 8 : h * 8 + 8, :] = v[:, b * 32 : b * 32 + 32]
-    for i in range(2):
-        v = fin[18 + i] * (float(TOTAL) ** -0.5)
-        for k in range(16 if i == 0 else 11):
-            w1_out[i * 16 + k] = v[(k // 8) * 4 : (k // 8) * 4 + 4, (k % 8) * 16 : (k % 8) * 16 + 16]
+    t4(1 - core).wait_recv()
+    fin_copy = pltpu.make_async_copy(fin, fin_h, o_sem.at[1])
+    fin_copy.start()
 
     for c in g_copies + i_copies + k_copies:
         c.wait_send()
@@ -432,20 +521,55 @@
             def _():
                 p3(n).wait_send()
 
+    t1().wait_send()
+    for n in range(16):
+        @pl.when(chip != n)
+        def _():
+            t2(n, chip).wait_send()
+    for n in range(8):
+        @pl.when(zc != n)
+        def _():
+            t3(n, zc).wait_send()
+    t4(core).wait_send()
+    gp_copy.wait()
+    fin_copy.wait()
+
+
+def finish(gp, fin, gp_out, w1_out, w2_out):
+    gp_out[...] = gp[...]
+    for o9 in range(9):
+        for h in range(2):
+            v = fin[2 * o9 + h] * (float(TOTAL // 8) ** -0.5)
+            for b in range(3):
+                w2_out[o9 * 3 + b, h * 8 : h * 8 + 8, :] = v[:, b * 32 : b * 32 + 32]
+    for i in range(2):
+        v = fin[TILES + i] * (float(TOTAL) ** -0.5)
+        for c in range(4):
+            w1_out[c, i * 8 : i * 8 + 8, :] = v[:, c * 32 : c * 32 + 27]
+
 
 def local(inputs, mask_one, place_one, pooled_one, w_two, mask_two, place_two, grad_two):
     vm = pl.BlockSpec(memory_space=pltpu.VMEM)
+    anywhere = pl.BlockSpec(memory_space=pl.ANY)
     dma = pltpu.SemaphoreType.DMA
-    gp, w1, w2 = pl.pallas_call(
+    gp, fin = pl.pallas_call(
         kernel,
         out_shape=(
             jax.ShapeDtypeStruct((48, 1024), BF16),
-            jax.ShapeDtypeStruct((27, 4, 16), F32),
-            jax.ShapeDtypeStruct((27, 16, 32), F32),
+            jax.ShapeDtypeStruct((TILES + 2, 8, 128), F32),
         ),
-        in_specs=[vm] * 8,
-        out_specs=(vm, vm, vm),
+        in_specs=[anywhere] * 8,
+        out_specs=(anywhere, anywhere),
         scratch_shapes=[
+            pltpu.VMEM((S, 4, 8192), BF16),
+            pltpu.VMEM((48, 8192), I32),
+            pltpu.VMEM((48, 1024), I32),
+            pltpu.VMEM((48, 1024), BF16),
+            pltpu.VMEM((27, 16, 32), BF16),
+            pltpu.VMEM((96, 1024), I32),
+            pltpu.VMEM((96, 128), I32),
+            pltpu.VMEM((96, 128), BF16),
+            pltpu.VMEM((48, 1024), BF16),
             pltpu.VMEM((2, 96, 128), BF16),
             pltpu.VMEM((2, 96, 128), BF16),
             pltpu.VMEM((2, 16, 128), BF16),
@@ -465,13 +589,20 @@
             pltpu.VMEM((18, 144, 256), BF16),
             pltpu.VMEM((48, 8192), BF16),
             pltpu.VMEM((S, 4, 128, 256), BF16),
-            pltpu.VMEM((432, 128), F32),
+            pltpu.VMEM((128, 432), F32),
             pltpu.VMEM((TILES, 8, 128), F32),
             pltpu.VMEM((32, 8, 128), F32),
             pltpu.VMEM((8, 8, 128), F32),
-            pltpu.VMEM((TILES, 8, 128), F32),
+            pltpu.VMEM((TILES + 2, 8, 128), F32),
+            pltpu.VMEM((3, 432, 128), BF16),
+            pltpu.VMEM((2, 8, 128), F32),
+            pltpu.VMEM((8, 128), F32),
+            pltpu.VMEM((16, 8, 128), F32),
+            pltpu.VMEM((8, 8, 128), F32),
             dma((26,)), dma((26,)), dma((8,)), dma((8,)), dma((2,)), dma((2,)),
             dma((TILES,)), dma((32,)), dma((8,)), dma((8,)), dma((32,)), dma((TILES,)),
+            dma, dma, dma((16,)), dma((16,)), dma((8,)), dma((8,)), dma, dma,
+            dma((8,)), dma((2,)),
         ],
         compiler_params=pltpu.CompilerParams(
             collective_id=0, has_side_effects=True, vmem_limit_bytes=56 * 1024 * 1024
@@ -487,7 +618,18 @@
         place_two.reshape(96, 128),
         grad_two.reshape(96, 128),
     )
-    return gp.reshape(S, 1, 16, 1024), w1, w2
+    gp, w1, w2 = pl.pallas_call(
+        finish,
+        out_shape=(
+            jax.ShapeDtypeStruct((48, 1024), BF16),
+            jax.ShapeDtypeStruct((4, 16, 27), F32),
+            jax.ShapeDtypeStruct((27, 16, 32), F32),
+        ),
+        in_specs=[vm, vm],
+        out_specs=(vm, vm, vm),
+        name="finish",
+    )(gp, fin)
+    return gp.reshape(S, 1, 16, 1024), w1.transpose(2, 0, 1), w2
 
 
 def solution(mesh):

time: 54 us -> 49.6 us (0.919)
  local copies, waits for them, and re-layouts: 4.69 us -> 0 us
    unnamed x3 -> x0, local copies, waits for them, and re-layouts: 4.69 us -> none
    pallas_call x0 -> x1, Pallas kernels: none -> 1.73 us  [local(): pl.pallas_call(finish, out_shape=(jax.ShapeDtypeStruct((48, 1024), BF16),...]
    pallas_call x1, Pallas kernels: 48.4 us -> 47.1 us  [local(): pl.pallas_call(kernel, out_shape=(jax.ShapeDtypeStruct((48, 1024), BF16),...]
where the time goes in v1:
time: 49.6 us; the launch traced here: 49.5 us
  Pallas kernels  48.8 us (98%)
  between operations  0.64 us (1%)
    pallas_call x1, Pallas kernels, local(): pl.pallas_call(kernel, out_shape=(jax.ShapeDtypeStruct((48, 1024), BF16),...  47.1 us
    pallas_call x1, Pallas kernels, local(): pl.pallas_call(finish, out_shape=(jax.ShapeDtypeStruct((48, 1024), BF16),...  1.73 us

profile of v1, /device:TPU:1, one launch (start us, length us, event | category | flops | bytes accessed | tf_op | source)
XLA Modules:
  0.0 49.5 jit_solution(1261495454788384068)
XLA Ops:
  0.6 47.1 %whole.1 = (bf16[48,1024]{1,0:T(8,128)(2,1)}, f32[20,8,128]{2,1,0:T(8,128)}) custom-call(bf16[3,4,8192]{2,1,0:T(4,128)(2,1)} %bitcast.13, s32[48,8192]{1,0:T(8,128)} %bitcast.11, s32[48,1024]{1,0:T(8,128)} %bitcast.14, bf16[48,1024]{1,0:T(8,128)(2,1)} %bitcast.15, bf16[27,16,32]{2,1,0:T(8,128)(2,1)} %w_two_h.1, s32[96,1024]{1,0:T(8,128)} %bitcast.12, ...), custom_call_target="tpu_custom_call" | custom-call | tf_op jit(solution)/shard_map/whole/pallas_call | solution.py:555
  47.7 1.7 %finish.1 = (bf16[48,1024]{1,0:T(8,128)(2,1)}, f32[4,16,27]{2,1,0:T(8,128)}, f32[27,16,32]{2,1,0:T(8,128)}) custom-call(bf16[48,1024]{1,0:T(8,128)(2,1)} %get-tuple-element.8.gp, f32[20,8,128]{2,1,0:T(8,128)} %get-tuple-element.9.fin), custom_call_target="tpu_custom_call" | custom-call | tf_op jit(solution)/shard_map/finish/pallas_call | solution.py:621

commit v2 on v1

--- a/solution.py
+++ b/solution.py
@@ -19,6 +19,7 @@
     for dk in (-1, 0, 1)
     if (di, dj, dk) != (0, 0, 0)
 ]
+GREETED = [(-1, 0, 0), (1, 0, 0), (0, 0, -1), (0, 0, 1)]
 XY = [(di, dj) for di in (-1, 0, 1) for dj in (-1, 0, 1) if (di, dj) != (0, 0)]
 NT = (((1,), (1,)), ((), ()))
 NN = (((1,), (0,)), ((), ()))
@@ -44,7 +45,8 @@
     mp, yb, tk, rx, ry, rt, z3, wp, pst, tbuf,
     iyb, rix, riy, in32, ko, rk, lhs, sel, gc, acc1,
     wg, r1, r2, fin, qbuf, own1, c1, c2, c3,
-    g_send, g_recv, i_send, i_recv, k_send, k_recv,
+    gx_send, gx_recv, gy_send, gy_recv, gt_send, gt_recv,
+    ix_send, ix_recv, iy_send, iy_recv, k_send, k_recv,
     s1_send, s1_recv, s2_send, s2_recv, s3_send, s3_recv,
     t1_send, t1_recv, t2_send, t2_recv, t3_send, t3_recv, t4_send, t4_recv,
     l_sem, o_sem,
@@ -54,6 +56,10 @@
     bi, bj, bk = sp // 16, (sp // 4) % 4, sp % 4
     zc, t8 = sp // 8, sp % 8
     men = dp * 8 + t8
+    core = dp % 2
+    chip = (dp // 2) * 8 + t8
+    owner = ((core == 0) & (chip < 9)) | ((core == 1) & (chip >= 7))
+    mine = jnp.where(core == 0, chip, chip + 2)
 
     def near(di, dj, dk):
         other = ((bi + di + 4) % 4) * 16 + ((bj + dj + 4) % 4) * 4 + (bk + dk + 4) % 4
@@ -65,48 +71,34 @@
     def column(zz):
         return {"space": zz * 8 + t8}
 
-    def p1(o):
-        return pltpu.make_async_remote_copy(
-            src_ref=wg.at[o], dst_ref=r1.at[men], send_sem=s1_send.at[o], recv_sem=s1_recv.at[men],
-            device_id=plane(o), device_id_type=MESH,
-        )
-
-    def p1_from(n):
-        return pltpu.make_async_remote_copy(
-            src_ref=wg.at[0], dst_ref=r1.at[n], send_sem=s1_send.at[0], recv_sem=s1_recv.at[n],
-            device_id=plane(n), device_id_type=MESH,
-        )
-
-    def p2(zz):
-        return pltpu.make_async_remote_copy(
-            src_ref=r2.at[zc], dst_ref=r2.at[zc], send_sem=s2_send.at[zz], recv_sem=s2_recv.at[zc],
-            device_id=column(zz), device_id_type=MESH,
-        )
-
-    def p2_from(zz):
-        return pltpu.make_async_remote_copy(
-            src_ref=r2.at[zz], dst_ref=r2.at[zz], send_sem=s2_send.at[zz], recv_sem=s2_recv.at[zz],
-            device_id=column(zz), device_id_type=MESH,
-        )
-
-    def p3(n):
-        return pltpu.make_async_remote_copy(
-            src_ref=fin.at[men], dst_ref=fin.at[men], send_sem=s3_send.at[n], recv_sem=s3_recv.at[men],
-            device_id=plane(n), device_id_type=MESH,
-        )
-
-    def p3_from(o):
-        return pltpu.make_async_remote_copy(
-            src_ref=fin.at[o], dst_ref=fin.at[o], send_sem=s3_send.at[0], recv_sem=s3_recv.at[o],
-            device_id=plane(o), device_id_type=MESH,
-        )
-
-    core = dp % 2
-    chip = (dp // 2) * 8 + t8
-
     def twin():
         return {"dp": dp + 1 - 2 * core}
 
+    def owner_of(o):
+        n = o if o < 9 else o - 2
+        return {"dp": (n // 8) * 2 + (0 if o < 9 else 1), "space": zc * 8 + n % 8}
+
+    def is_mine(o):
+        return owner & (mine == o)
+
+    def p1(o):
+        return pltpu.make_async_remote_copy(
+            src_ref=wg.at[o], dst_ref=r1.at[men], send_sem=s1_send, recv_sem=s1_recv,
+            device_id=owner_of(o), device_id_type=MESH,
+        )
+
+    def p2(n):
+        return pltpu.make_async_remote_copy(
+            src_ref=r2.at[zc], dst_ref=r2.at[zc], send_sem=s2_send, recv_sem=s2_recv,
+            device_id=column((zc + n) % 8), device_id_type=MESH,
+        )
+
+    def p3(n):
+        return pltpu.make_async_remote_copy(
+            src_ref=fin.at[mine], dst_ref=fin.at[mine], send_sem=s3_send, recv_sem=s3_recv,
+            device_id=plane((men + n) % 32), device_id_type=MESH,
+        )
+
     def chip_at(n):
         return {"dp": (n // 8) * 2 + core, "space": zc * 8 + n % 8}
 
@@ -116,16 +108,16 @@
             device_id=twin(), device_id_type=MESH,
         )
 
-    def t2(n, slot):
-        return pltpu.make_async_remote_copy(
-            src_ref=c2.at[slot], dst_ref=c2.at[slot], send_sem=t2_send.at[n], recv_sem=t2_recv.at[slot],
-            device_id=chip_at(n), device_id_type=MESH,
-        )
-
-    def t3(n, slot):
-        return pltpu.make_async_remote_copy(
-            src_ref=c3.at[slot], dst_ref=c3.at[slot], send_sem=t3_send.at[n], recv_sem=t3_recv.at[slot],
-            device_id=column(n), device_id_type=MESH,
+    def t2(n):
+        return pltpu.make_async_remote_copy(
+            src_ref=c2.at[chip], dst_ref=c2.at[chip], send_sem=t2_send, recv_sem=t2_recv,
+            device_id=chip_at((chip + n) % 16), device_id_type=MESH,
+        )
+
+    def t3(n):
+        return pltpu.make_async_remote_copy(
+            src_ref=c3.at[zc], dst_ref=c3.at[zc], send_sem=t3_send, recv_sem=t3_recv,
+            device_id=column((zc + n) % 8), device_id_type=MESH,
         )
 
     def t4(slot):
@@ -133,6 +125,24 @@
             src_ref=fin.at[TILES + slot], dst_ref=fin.at[TILES + slot], send_sem=t4_send, recv_sem=t4_recv,
             device_id=twin(), device_id_type=MESH,
         )
+
+    def group(ref, send_sem, recv_sem):
+        return pltpu.make_async_remote_copy(
+            src_ref=ref, dst_ref=ref, send_sem=send_sem, recv_sem=recv_sem,
+            device_id=twin(), device_id_type=MESH,
+        )
+
+    gx_all, gy_all, gt_all = group(rx, gx_send, gx_recv), group(ry, gy_send, gy_recv), group(rt, gt_send, gt_recv)
+    ix_all, iy_all, k_all = group(rix, ix_send, ix_recv), group(riy, iy_send, iy_recv), group(rk, k_send, k_recv)
+    p1_got = group(r1.at[0:31], s1_send, s1_recv)
+    p1_sent = group(wg.at[0 : TILES - 1], s1_send, s1_recv)
+    p1_sent_all = group(wg, s1_send, s1_recv)
+    p2_all = group(r2.at[0:7], s2_send, s2_recv)
+    p3_sent = group(r1.at[0:31], s3_send, s3_recv)
+    p3_got = group(fin.at[0 : TILES - 1], s3_send, s3_recv)
+    p3_got_all = group(fin.at[0:TILES], s3_send, s3_recv)
+    t2_all = group(c2.at[0:15], t2_send, t2_recv)
+    t3_all = group(c3.at[0:7], t3_send, t3_recv)
 
     loads = [
         pltpu.make_async_copy(a, b, l_sem.at[n])
@@ -154,6 +164,8 @@
 
     barrier = pltpu.get_barrier_semaphore()
     for d in NEIGHBOURS:
+        if d in GREETED:
+            continue
         pl.semaphore_signal(barrier, inc=1, device_id=near(*d), device_id_type=MESH)
     for n in range(1, 32):
         pl.semaphore_signal(barrier, inc=1, device_id=plane((men + n) % 32), device_id_type=MESH)
@@ -197,20 +209,23 @@
             at = x * 2048 + y * 256
             iyb[q, :, :, x * 256 : (x + 1) * 256] = inp[:, :, at : at + 256]
 
-    pl.semaphore_wait(barrier, 64)
+    pl.semaphore_wait(barrier, 60)
 
     def g_copy(n, d):
         di, dj, dk = d
         if dk != 0:
             src = tk.at[0 if dk > 0 else 1]
             dst = rt.at[(1 - di) * 3 + 1 - dj, 0 if dk > 0 else 1]
+            sems = gt_send, gt_recv
         elif dj == 0:
             src, dst = mp, rx.at[(1 - di) // 2]
+            sems = gx_send, gx_recv
         else:
             src = yb.at[(1 + dj) // 2]
             dst = ry.at[1 - di, (1 - dj) // 2]
-        return pltpu.make_async_remote_copy(
-            src_ref=src, dst_ref=dst, send_sem=g_send.at[n], recv_sem=g_recv.at[n],
+            sems = gy_send, gy_recv
+        return pltpu.make_async_remote_copy(
+            src_ref=src, dst_ref=dst, send_sem=sems[0], recv_sem=sems[1],
             device_id=near(*d), device_id_type=MESH,
         )
 
@@ -219,8 +234,10 @@
         if dj == 0:
             at = 3 * 2048 if di > 0 else 0
             src, dst = inp.at[:, :, at : at + 2048], rix.at[(1 - di) // 2]
+            sems = ix_send, ix_recv
         else:
             q = (1 + dj) // 2
+            sems = iy_send, iy_recv
             if di == 0:
                 src = iyb.at[q]
                 dst = riy.at[(1 - dj) // 2, :, :, 256 : 256 + 1024]
@@ -230,7 +247,7 @@
                 src = iyb.at[q, :, :, at : at + 256]
                 dst = riy.at[(1 - dj) // 2, :, :, to : to + 256]
         return pltpu.make_async_remote_copy(
-            src_ref=src, dst_ref=dst, send_sem=i_send.at[n], recv_sem=i_recv.at[n],
+            src_ref=src, dst_ref=dst, send_sem=sems[0], recv_sem=sems[1],
             device_id=near(di, dj, 0), device_id_type=MESH,
         )
 
@@ -280,8 +297,8 @@
                     ok = (up == par1 + float(4 * dx + 2 * dy)) & (mask_one[:, to : to + 256] == 1)
                     sel[:, to : to + 256] = one_hot(ok)
 
-    for n in range(26):
-        g_copies[n].wait_recv()
+    for c in (gt_all, gx_all, gy_all):
+        c.wait_recv()
     fr, fc = iota((32, 768), 0), iota((32, 768), 1)
     f_in, f_mid, f_b = fc % 128, (fc // 128) % 2, fc // 256
     left = (f_b == 2) & (f_in == 0)
@@ -330,7 +347,7 @@
     for i in range(TILES):
         wg[i] = w2[i * 8 : i * 8 + 8]
     for o in range(TILES):
-        @pl.when(men != o)
+        @pl.when(~is_mine(o))
         def _():
             p1(o).start()
 
@@ -349,8 +366,8 @@
     gp_copy = pltpu.make_async_copy(gp, gp_h, o_sem.at[0])
     gp_copy.start()
 
-    for n in range(8):
-        i_copies[n].wait_recv()
+    for c in (ix_all, iy_all):
+        c.wait_recv()
     in32[...] = jnp.zeros_like(in32)
     for s in range(S):
         for x in range(6):
@@ -377,7 +394,7 @@
     def k_copy(side):
         return pltpu.make_async_remote_copy(
             src_ref=ko.at[side], dst_ref=rk.at[side],
-            send_sem=k_send.at[side], recv_sem=k_recv.at[side],
+            send_sem=k_send, recv_sem=k_recv,
             device_id=near(0, 0, 1 if side == 0 else -1), device_id_type=MESH,
         )
 
@@ -385,8 +402,7 @@
     for c in k_copies:
         c.start()
 
-    for c in k_copies:
-        c.wait_recv()
+    k_all.wait_recv()
     lane256 = iota((48, 256), 1)
     for l in range(18):
         v = in32[l]
@@ -433,104 +449,74 @@
     own1[1] = w1[8:16]
 
     t1().start()
-    owner = men < TILES
 
     @pl.when(owner)
     def _():
-        r1[men] = wg[men]
-        for n in range(32):
-            @pl.when(men != n)
-            def _():
-                p1_from(n).wait_recv()
+        p1_got.wait_recv()
+        r1[men] = wg[mine]
         total = r1[0]
         for n in range(1, 32):
             total = total + r1[n]
         r2[zc] = total
-        for zz in range(8):
-            @pl.when(zc != zz)
-            def _():
-                p2(zz).start()
+        for n in range(1, 8):
+            p2(n).start()
 
     t1().wait_recv()
     c2[chip] = own1[core] + c1[...]
-    for n in range(16):
-        @pl.when(chip != n)
-        def _():
-            t2(n, chip).start()
+    for n in range(1, 16):
+        t2(n).start()
 
     @pl.when(owner)
     def _():
-        for zz in range(8):
-            @pl.when(zc != zz)
-            def _():
-                p2_from(zz).wait_recv()
+        p2_all.wait_recv()
         total = r2[0]
         for zz in range(1, 8):
             total = total + r2[zz]
-        fin[men] = total
-        for n in range(32):
-            @pl.when(men != n)
-            def _():
-                p3(n).start()
-
-    for n in range(16):
-        @pl.when(chip != n)
-        def _():
-            t2(n, n).wait_recv()
+        fin[mine] = total
+        for n in range(1, 32):
+            p3(n).start()
+
+    t2_all.wait_recv()
     total = c2[0]
     for n in range(1, 16):
         total = total + c2[n]
     c3[zc] = total
-    for n in range(8):
-        @pl.when(zc != n)
-        def _():
-            t3(n, zc).start()
-    for n in range(8):
-        @pl.when(zc != n)
-        def _():
-            t3(n, n).wait_recv()
+    for n in range(1, 8):
+        t3(n).start()
+    t3_all.wait_recv()
     total = c3[0]
     for n in range(1, 8):
         total = total + c3[n]
     fin[TILES + core] = total
     t4(core).start()
 
-    for o in range(TILES):
-        @pl.when(men != o)
-        def _():
-            p3_from(o).wait_recv()
+    @pl.when(owner)
+    def _():
+        p3_got.wait_recv()
+
+    @pl.when(~owner)
+    def _():
+        p3_got_all.wait_recv()
+
     t4(1 - core).wait_recv()
     fin_copy = pltpu.make_async_copy(fin, fin_h, o_sem.at[1])
     fin_copy.start()
 
-    for c in g_copies + i_copies + k_copies:
+    for c in (gt_all, gx_all, gy_all, ix_all, iy_all, k_all, t2_all, t3_all):
         c.wait_send()
-    for o in range(TILES):
-        @pl.when(men != o)
-        def _():
-            p1(o).wait_send()
+    t1().wait_send()
+    t4(core).wait_send()
 
     @pl.when(owner)
     def _():
-        for zz in range(8):
-            @pl.when(zc != zz)
-            def _():
-                p2(zz).wait_send()
-        for n in range(32):
-            @pl.when(men != n)
-            def _():
-                p3(n).wait_send()
-
-    t1().wait_send()
-    for n in range(16):
-        @pl.when(chip != n)
-        def _():
-            t2(n, chip).wait_send()
-    for n in range(8):
-        @pl.when(zc != n)
-        def _():
-            t3(n, zc).wait_send()
-    t4(core).wait_send()
+        p1_sent.wait_send()
+        p2_all.wait_send()
+        p3_sent.wait_send()
+
+    @pl.when(~owner)
+    def _():
+        p1_sent_all.wait_send()
+
     gp_copy.wait()
     fin_copy.wait()
 
@@ -599,9 +585,9 @@
             pltpu.VMEM((8, 128), F32),
             pltpu.VMEM((16, 8, 128), F32),
             pltpu.VMEM((8, 8, 128), F32),
-            dma((26,)), dma((26,)), dma((8,)), dma((8,)), dma((2,)), dma((2,)),
-            dma((TILES,)), dma((32,)), dma((8,)), dma((8,)), dma((32,)), dma((TILES,)),
-            dma, dma, dma((16,)), dma((16,)), dma((8,)), dma((8,)), dma, dma,
+            *[dma] * 12,
+            *[dma] * 6,
+            *[dma] * 8,
             dma((8,)), dma((2,)),
         ],
         compiler_params=pltpu.CompilerParams(

time: 49.6 us -> 47.7 us (0.962)
  Pallas kernels: 48.8 us -> 47 us
    pallas_call x1, Pallas kernels: 47.1 us -> 45.2 us  [local(): pl.pallas_call(kernel, out_shape=(jax.ShapeDtypeStruct((48, 1024), BF16),...]
where the time goes in v2:
time: 47.7 us; the launch traced here: 47.6 us
  Pallas kernels  47 us (99%)
  between operations  0.64 us (1%)
    pallas_call x1, Pallas kernels, local(): pl.pallas_call(kernel, out_shape=(jax.ShapeDtypeStruct((48, 1024), BF16),...  45.2 us
    pallas_call x1, Pallas kernels, local(): pl.pallas_call(finish, out_shape=(jax.ShapeDtypeStruct((48, 1024), BF16),...  1.73 us

profile of v2, /device:TPU:1, one launch (start us, length us, event | category | flops | bytes accessed | tf_op | source)
XLA Modules:
  0.0 47.6 jit_solution(8615887373918280527)
XLA Ops:
  0.6 45.2 %whole.1 = (bf16[48,1024]{1,0:T(8,128)(2,1)}, f32[20,8,128]{2,1,0:T(8,128)}) custom-call(bf16[3,4,8192]{2,1,0:T(4,128)(2,1)} %bitcast.13, s32[48,8192]{1,0:T(8,128)} %bitcast.11, s32[48,1024]{1,0:T(8,128)} %bitcast.14, bf16[48,1024]{1,0:T(8,128)(2,1)} %bitcast.15, bf16[27,16,32]{2,1,0:T(8,128)(2,1)} %w_two_h.1, s32[96,1024]{1,0:T(8,128)} %bitcast.12, ...), custom_call_target="tpu_custom_call" | custom-call | tf_op jit(solution)/shard_map/whole/pallas_call | solution.py:541
  45.9 1.7 %finish.1 = (bf16[48,1024]{1,0:T(8,128)(2,1)}, f32[4,16,27]{2,1,0:T(8,128)}, f32[27,16,32]{2,1,0:T(8,128)}) custom-call(bf16[48,1024]{1,0:T(8,128)(2,1)} %get-tuple-element.8.gp, f32[20,8,128]{2,1,0:T(8,128)} %get-tuple-element.9.fin), custom_call_target="tpu_custom_call" | custom-call | tf_op jit(solution)/shard_map/finish/pallas_call | solution.py:607

commit v3 on v2

--- a/solution.py
+++ b/solution.py
@@ -44,11 +44,11 @@
     inp, mask_one, place_one, pooled, w_two, mask_two, place_two, grad_two, gp,
     mp, yb, tk, rx, ry, rt, z3, wp, pst, tbuf,
     iyb, rix, riy, in32, ko, rk, lhs, sel, gc, acc1,
-    wg, r1, r2, fin, qbuf, own1, c1, c2, c3,
+    wg, r1, r2, fin, qbuf, ca, cb, cc,
     gx_send, gx_recv, gy_send, gy_recv, gt_send, gt_recv,
     ix_send, ix_recv, iy_send, iy_recv, k_send, k_recv,
     s1_send, s1_recv, s2_send, s2_recv, s3_send, s3_recv,
-    t1_send, t1_recv, t2_send, t2_recv, t3_send, t3_recv, t4_send, t4_recv,
+    s4_send, s4_recv, ta_send, ta_recv, tb_send, tb_recv, tc_send, tc_recv,
     l_sem, o_sem,
 ):
     dp = lax.axis_index("dp")
@@ -96,34 +96,41 @@
     def p3(n):
         return pltpu.make_async_remote_copy(
             src_ref=fin.at[mine], dst_ref=fin.at[mine], send_sem=s3_send, recv_sem=s3_recv,
-            device_id=plane((men + n) % 32), device_id_type=MESH,
+            device_id=chip_at((chip + n) % 16), device_id_type=MESH,
+        )
+
+    def p4(half):
+        nine = fin.at[pl.ds(half * 9, 9)]
+        return pltpu.make_async_remote_copy(
+            src_ref=nine, dst_ref=nine, send_sem=s4_send, recv_sem=s4_recv,
+            device_id=twin(), device_id_type=MESH,
         )
 
     def chip_at(n):
         return {"dp": (n // 8) * 2 + core, "space": zc * 8 + n % 8}
 
-    def t1():
-        return pltpu.make_async_remote_copy(
-            src_ref=own1.at[1 - core], dst_ref=c1, send_sem=t1_send, recv_sem=t1_recv,
-            device_id=twin(), device_id_type=MESH,
-        )
-
-    def t2(n):
-        return pltpu.make_async_remote_copy(
-            src_ref=c2.at[chip], dst_ref=c2.at[chip], send_sem=t2_send, recv_sem=t2_recv,
-            device_id=chip_at((chip + n) % 16), device_id_type=MESH,
-        )
-
-    def t3(n):
-        return pltpu.make_async_remote_copy(
-            src_ref=c3.at[zc], dst_ref=c3.at[zc], send_sem=t3_send, recv_sem=t3_recv,
+    y_lo, y_hi, x4 = dp // 2, t8 // 4, t8 % 4
+    me_a = core * 4 + x4
+    me_b = y_lo * 2 + y_hi
+
+    def ta(n):
+        a = (me_a + n) % 8
+        return pltpu.make_async_remote_copy(
+            src_ref=ca.at[me_a], dst_ref=ca.at[me_a], send_sem=ta_send, recv_sem=ta_recv,
+            device_id={"dp": y_lo * 2 + a // 4, "space": zc * 8 + y_hi * 4 + a % 4}, device_id_type=MESH,
+        )
+
+    def tb(n):
+        b = (me_b + n) % 4
+        return pltpu.make_async_remote_copy(
+            src_ref=cb.at[me_b], dst_ref=cb.at[me_b], send_sem=tb_send, recv_sem=tb_recv,
+            device_id={"dp": (b // 2) * 2 + core, "space": zc * 8 + (b % 2) * 4 + x4}, device_id_type=MESH,
+        )
+
+    def tc_(n):
+        return pltpu.make_async_remote_copy(
+            src_ref=cc.at[zc], dst_ref=cc.at[zc], send_sem=tc_send, recv_sem=tc_recv,
             device_id=column((zc + n) % 8), device_id_type=MESH,
-        )
-
-    def t4(slot):
-        return pltpu.make_async_remote_copy(
-            src_ref=fin.at[TILES + slot], dst_ref=fin.at[TILES + slot], send_sem=t4_send, recv_sem=t4_recv,
-            device_id=twin(), device_id_type=MESH,
         )
 
     def group(ref, send_sem, recv_sem):
@@ -138,11 +145,22 @@
     p1_sent = group(wg.at[0 : TILES - 1], s1_send, s1_recv)
     p1_sent_all = group(wg, s1_send, s1_recv)
     p2_all = group(r2.at[0:7], s2_send, s2_recv)
-    p3_sent = group(r1.at[0:31], s3_send, s3_recv)
-    p3_got = group(fin.at[0 : TILES - 1], s3_send, s3_recv)
-    p3_got_all = group(fin.at[0:TILES], s3_send, s3_recv)
-    t2_all = group(c2.at[0:15], t2_send, t2_recv)
-    t3_all = group(c3.at[0:7], t3_send, t3_recv)
+    p3_sent = group(r1.at[0:15], s3_send, s3_recv)
+    p3_got = group(fin.at[0:8], s3_send, s3_recv)
+    p3_got_all = group(fin.at[0:9], s3_send, s3_recv)
+    ta_all = group(ca.at[0:7], ta_send, ta_recv)
+    tb_all = group(cb.at[0:3], tb_send, tb_recv)
+    tc_all = group(cc.at[0:7], tc_send, tc_recv)
+
+    barrier = pltpu.get_barrier_semaphore()
+    for d in sorted(NEIGHBOURS, key=lambda d: -3 * abs(d[1]) - 2 * abs(d[0]) - abs(d[2])):
+        if d in GREETED:
+            continue
+        pl.semaphore_signal(barrier, inc=1, device_id=near(*d), device_id_type=MESH)
+    for n in range(1, 32):
+        pl.semaphore_signal(barrier, inc=1, device_id=plane((men + n) % 32), device_id_type=MESH)
+    for n in range(1, 8):
+        pl.semaphore_signal(barrier, inc=1, device_id=column((zc + n) % 8), device_id_type=MESH)
 
     loads = [
         pltpu.make_async_copy(a, b, l_sem.at[n])
@@ -161,16 +179,6 @@
     ]
     for c in loads:
         c.start()
-
-    barrier = pltpu.get_barrier_semaphore()
-    for d in NEIGHBOURS:
-        if d in GREETED:
-            continue
-        pl.semaphore_signal(barrier, inc=1, device_id=near(*d), device_id_type=MESH)
-    for n in range(1, 32):
-        pl.semaphore_signal(barrier, inc=1, device_id=plane((men + n) % 32), device_id_type=MESH)
-    for n in range(1, 8):
-        pl.semaphore_signal(barrier, inc=1, device_id=column((zc + n) % 8), device_id_type=MESH)
 
     er, ec = iota((128, 768), 0), iota((128, 768), 1)
     ez = ec % 128 - (ec // 256 - 1)
@@ -297,8 +305,6 @@
                     ok = (up == par1 + float(4 * dx + 2 * dy)) & (mask_one[:, to : to + 256] == 1)
                     sel[:, to : to + 256] = one_hot(ok)
 
-    for c in (gt_all, gx_all, gy_all):
-        c.wait_recv()
     fr, fc = iota((32, 768), 0), iota((32, 768), 1)
     f_in, f_mid, f_b = fc % 128, (fc // 128) % 2, fc // 256
     left = (f_b == 2) & (f_in == 0)
@@ -311,6 +317,7 @@
     f_y = [halo_rows(2 * f_mid + q) for q in range(2)]
     lane = (iota((96, 128), 1) % 2).astype(F32)
     dz = [1.0 - lane, lane, 1.0 - lane]
+    gt_all.wait_recv()
 
     def put(b, x, y, dx, dy, um, up):
         v = jnp.where(up == dz[b] + float(4 * dx + 2 * dy), um, 0.0).astype(BF16)
@@ -318,8 +325,12 @@
         for s in range(S):
             z3[s, b * 32 : b * 32 + 32, to : to + 128] = v[s * 32 : s * 32 + 32]
 
-    for di in (-1, 0, 1):
-        for dj in (-1, 0, 1):
+    for dj in (0, -1, 1):
+        if dj == -1:
+            gy_all.wait_recv()
+        for di in (0, -1, 1):
+            if dj == 0 and di == -1:
+                gx_all.wait_recv()
             stack = rt[(di + 1) * 3 + dj + 1].reshape(32, 128)[:, 0:96]
             xs = {-1: [(0, 1)], 0: [(1, 0), (2, 1)], 1: [(3, 0)]}[di]
             if dj == 0:
@@ -402,16 +413,6 @@
     for c in k_copies:
         c.start()
 
-    k_all.wait_recv()
-    lane256 = iota((48, 256), 1)
-    for l in range(18):
-        v = in32[l]
-        below = jnp.concatenate([pltpu.roll(rk[0], (0 - l) % 128, 1), jnp.zeros((48, 128), F32)], axis=1)
-        above = jnp.concatenate([jnp.zeros((48, 128), F32), pltpu.roll(rk[1], (127 - l) % 128, 1)], axis=1)
-        lhs[l, 0:48, :] = jnp.where(lane256 == 0, below, pltpu.roll(v, 1, 1)).astype(BF16)
-        lhs[l, 48:96, :] = v.astype(BF16)
-        lhs[l, 96:144, :] = jnp.where(lane256 == 255, above, pltpu.roll(v, 255, 1)).astype(BF16)
-
     for hx in range(2):
         for hy in range(4):
             at = (hx * 4 + hy) * 128
@@ -423,6 +424,27 @@
                     v = (up * sel[:, to : to + 256].astype(F32)).astype(BF16)
                     for s in range(S):
                         gc[s, x, y * 16 : y * 16 + 16, :] = v[s * 16 : s * 16 + 16]
+    @pl.when(owner)
+    def _():
+        p1_got.wait_recv()
+        r1[men] = wg[mine]
+        total = r1[0]
+        for n in range(1, 32):
+            total = total + r1[n]
+        r2[zc] = total
+        for n in range(1, 8):
+            p2(n).start()
+
+    k_all.wait_recv()
+    lane256 = iota((48, 256), 1)
+    for l in range(18):
+        v = in32[l]
+        below = jnp.concatenate([pltpu.roll(rk[0], (0 - l) % 128, 1), jnp.zeros((48, 128), F32)], axis=1)
+        above = jnp.concatenate([jnp.zeros((48, 128), F32), pltpu.roll(rk[1], (127 - l) % 128, 1)], axis=1)
+        lhs[l, 0:48, :] = jnp.where(lane256 == 0, below, pltpu.roll(v, 1, 1)).astype(BF16)
+        lhs[l, 48:96, :] = v.astype(BF16)
+        lhs[l, 96:144, :] = jnp.where(lane256 == 255, above, pltpu.roll(v, 255, 1)).astype(BF16)
+
     a1 = jnp.zeros((128, 432), F32)
     for s in range(S):
         for x in range(4):
@@ -445,26 +467,10 @@
         low_part = (t - mid.astype(F32)).astype(BF16)
         r = dot(jnp.concatenate([hi, mid, low_part], axis=0), qbuf[oy])
         w1 = w1 + (r[0:16] + r[16:32] + r[32:48])
-    own1[0] = w1[0:8]
-    own1[1] = w1[8:16]
-
-    t1().start()
-
-    @pl.when(owner)
-    def _():
-        p1_got.wait_recv()
-        r1[men] = wg[mine]
-        total = r1[0]
-        for n in range(1, 32):
-            total = total + r1[n]
-        r2[zc] = total
-        for n in range(1, 8):
-            p2(n).start()
-
-    t1().wait_recv()
-    c2[chip] = own1[core] + c1[...]
-    for n in range(1, 16):
-        t2(n).start()
+    ca[me_a, 0] = w1[0:8]
+    ca[me_a, 1] = w1[8:16]
+    for n in range(1, 8):
+        ta(n).start()
 
     @pl.when(owner)
     def _():
@@ -473,22 +479,23 @@
         for zz in range(1, 8):
             total = total + r2[zz]
         fin[mine] = total
-        for n in range(1, 32):
+        for n in range(1, 16):
             p3(n).start()
 
-    t2_all.wait_recv()
-    total = c2[0]
-    for n in range(1, 16):
-        total = total + c2[n]
-    c3[zc] = total
+    ta_all.wait_recv()
+    total = ca[0]
     for n in range(1, 8):
-        t3(n).start()
-    t3_all.wait_recv()
-    total = c3[0]
+        total = total + ca[n]
+    cb[me_b] = total
+    for n in range(1, 4):
+        tb(n).start()
+    tb_all.wait_recv()
+    total = cb[0]
+    for n in range(1, 4):
+        total = total + cb[n]
+    cc[zc] = total
     for n in range(1, 8):
-        total = total + c3[n]
-    fin[TILES + core] = total
-    t4(core).start()
+        tc_(n).start()
 
     @pl.when(owner)
     def _():
@@ -498,14 +505,20 @@
     def _():
         p3_got_all.wait_recv()
 
-    t4(1 - core).wait_recv()
+    p4(core).start()
+    tc_all.wait_recv()
+    total = cc[0]
+    for n in range(1, 8):
+        total = total + cc[n]
+    fin[TILES] = total[0]
+    fin[TILES + 1] = total[1]
+    p4(1 - core).wait_recv()
     fin_copy = pltpu.make_async_copy(fin, fin_h, o_sem.at[1])
     fin_copy.start()
 
-    for c in (gt_all, gx_all, gy_all, ix_all, iy_all, k_all, t2_all, t3_all):
+    for c in (gt_all, gx_all, gy_all, ix_all, iy_all, k_all, ta_all, tb_all, tc_all):
         c.wait_send()
-    t1().wait_send()
-    t4(core).wait_send()
+    p4(core).wait_send()
 
     @pl.when(owner)
     def _():
@@ -581,10 +594,9 @@
             pltpu.VMEM((8, 8, 128), F32),
             pltpu.VMEM((TILES + 2, 8, 128), F32),
             pltpu.VMEM((3, 432, 128), BF16),
-            pltpu.VMEM((2, 8, 128), F32),
-            pltpu.VMEM((8, 128), F32),
-            pltpu.VMEM((16, 8, 128), F32),
-            pltpu.VMEM((8, 8, 128), F32),
+            pltpu.VMEM((8, 2, 8, 128), F32),
+            pltpu.VMEM((4, 2, 8, 128), F32),
+            pltpu.VMEM((8, 2, 8, 128), F32),
             *[dma] * 12,
             *[dma] * 6,
             *[dma] * 8,

time: 47.7 us -> 47 us (0.985)
  Pallas kernels: 47 us -> 46 us
    pallas_call x1, Pallas kernels: 45.2 us -> 44.3 us  [local(): pl.pallas_call(kernel, out_shape=(jax.ShapeDtypeStruct((48, 1024), BF16),...]
where the time goes in v3:
time: 47 us; the launch traced here: 46.7 us
  Pallas kernels  46 us (98%)
  between operations  0.64 us (1%)
    pallas_call x1, Pallas kernels, local(): pl.pallas_call(kernel, out_shape=(jax.ShapeDtypeStruct((48, 1024), BF16),...  44.3 us
    pallas_call x1, Pallas kernels, local(): pl.pallas_call(finish, out_shape=(jax.ShapeDtypeStruct((48, 1024), BF16),...  1.73 us

profile of v3, /device:TPU:1, one launch (start us, length us, event | category | flops | bytes accessed | tf_op | source)
XLA Modules:
  0.0 46.7 jit_solution(14943025289904872896)
XLA Ops:
  0.6 44.3 %whole.1 = (bf16[48,1024]{1,0:T(8,128)(2,1)}, f32[20,8,128]{2,1,0:T(8,128)}) custom-call(bf16[3,4,8192]{2,1,0:T(4,128)(2,1)} %bitcast.13, s32[48,8192]{1,0:T(8,128)} %bitcast.11, s32[48,1024]{1,0:T(8,128)} %bitcast.14, bf16[48,1024]{1,0:T(8,128)(2,1)} %bitcast.15, bf16[27,16,32]{2,1,0:T(8,128)(2,1)} %w_two_h.1, s32[96,1024]{1,0:T(8,128)} %bitcast.12, ...), custom_call_target="tpu_custom_call" | custom-call | tf_op jit(solution)/shard_map/whole/pallas_call | solution.py:554
  44.9 1.7 %finish.1 = (bf16[48,1024]{1,0:T(8,128)(2,1)}, f32[4,16,27]{2,1,0:T(8,128)}, f32[27,16,32]{2,1,0:T(8,128)}) custom-call(bf16[48,1024]{1,0:T(8,128)(2,1)} %get-tuple-element.8.gp, f32[20,8,128]{2,1,0:T(8,128)} %get-tuple-element.9.fin), custom_call_target="tpu_custom_call" | custom-call | tf_op jit(solution)/shard_map/finish/pallas_call | solution.py:619

commit v4 on v3

--- a/solution.py
+++ b/solution.py
@@ -44,7 +44,7 @@
     inp, mask_one, place_one, pooled, w_two, mask_two, place_two, grad_two, gp,
     mp, yb, tk, rx, ry, rt, z3, wp, pst, tbuf,
     iyb, rix, riy, in32, ko, rk, lhs, sel, gc, acc1,
-    wg, r1, r2, fin, qbuf, ca, cb, cc,
+    wg, r1, r2, fin, qbuf, own1, c1, c2, c3,
     gx_send, gx_recv, gy_send, gy_recv, gt_send, gt_recv,
     ix_send, ix_recv, iy_send, iy_recv, k_send, k_recv,
     s1_send, s1_recv, s2_send, s2_recv, s3_send, s3_recv,
@@ -109,28 +109,22 @@
     def chip_at(n):
         return {"dp": (n // 8) * 2 + core, "space": zc * 8 + n % 8}
 
-    y_lo, y_hi, x4 = dp // 2, t8 // 4, t8 % 4
-    me_a = core * 4 + x4
-    me_b = y_lo * 2 + y_hi
-
-    def ta(n):
-        a = (me_a + n) % 8
-        return pltpu.make_async_remote_copy(
-            src_ref=ca.at[me_a], dst_ref=ca.at[me_a], send_sem=ta_send, recv_sem=ta_recv,
-            device_id={"dp": y_lo * 2 + a // 4, "space": zc * 8 + y_hi * 4 + a % 4}, device_id_type=MESH,
-        )
-
-    def tb(n):
-        b = (me_b + n) % 4
-        return pltpu.make_async_remote_copy(
-            src_ref=cb.at[me_b], dst_ref=cb.at[me_b], send_sem=tb_send, recv_sem=tb_recv,
-            device_id={"dp": (b // 2) * 2 + core, "space": zc * 8 + (b % 2) * 4 + x4}, device_id_type=MESH,
-        )
-
-    def tc_(n):
-        return pltpu.make_async_remote_copy(
-            src_ref=cc.at[zc], dst_ref=cc.at[zc], send_sem=tc_send, recv_sem=tc_recv,
-            device_id=column((zc + n) % 8), device_id_type=MESH,
+    def t1():
+        return pltpu.make_async_remote_copy(
+            src_ref=own1.at[1 - core], dst_ref=c1, send_sem=ta_send, recv_sem=ta_recv,
+            device_id=twin(), device_id_type=MESH,
+        )
+
+    def t2(n):
+        return pltpu.make_async_remote_copy(
+            src_ref=c2.at[chip], dst_ref=c2.at[chip], send_sem=tb_send, recv_sem=tb_recv,
+            device_id=chip_at((chip + n) % 16), device_id_type=MESH,
+        )
+
+    def t3(n, to):
+        return pltpu.make_async_remote_copy(
+            src_ref=c3.at[core, zc], dst_ref=c3.at[core, zc], send_sem=tc_send, recv_sem=tc_recv,
+            device_id={"dp": to, "space": ((zc + n) % 8) * 8 + t8}, device_id_type=MESH,
         )
 
     def group(ref, send_sem, recv_sem):
@@ -148,9 +142,8 @@
     p3_sent = group(r1.at[0:15], s3_send, s3_recv)
     p3_got = group(fin.at[0:8], s3_send, s3_recv)
     p3_got_all = group(fin.at[0:9], s3_send, s3_recv)
-    ta_all = group(ca.at[0:7], ta_send, ta_recv)
-    tb_all = group(cb.at[0:3], tb_send, tb_recv)
-    tc_all = group(cc.at[0:7], tc_send, tc_recv)
+    t2_all = group(c2.at[0:15], tb_send, tb_recv)
+    t3_all = group(c2.at[0:15], tc_send, tc_recv)
 
     barrier = pltpu.get_barrier_semaphore()
     for d in sorted(NEIGHBOURS, key=lambda d: -3 * abs(d[1]) - 2 * abs(d[0]) - abs(d[2])):
@@ -161,6 +154,8 @@
         pl.semaphore_signal(barrier, inc=1, device_id=plane((men + n) % 32), device_id_type=MESH)
     for n in range(1, 8):
         pl.semaphore_signal(barrier, inc=1, device_id=column((zc + n) % 8), device_id_type=MESH)
+        other = {"dp": dp + 1 - 2 * core, "space": ((zc + n) % 8) * 8 + t8}
+        pl.semaphore_signal(barrier, inc=1, device_id=other, device_id_type=MESH)
 
     loads = [
         pltpu.make_async_copy(a, b, l_sem.at[n])
@@ -217,7 +212,7 @@
             at = x * 2048 + y * 256
             iyb[q, :, :, x * 256 : (x + 1) * 256] = inp[:, :, at : at + 256]
 
-    pl.semaphore_wait(barrier, 60)
+    pl.semaphore_wait(barrier, 67)
 
     def g_copy(n, d):
         di, dj, dk = d
@@ -400,7 +395,7 @@
             tile = in32[l, :, 128:256] if side == 0 else in32[l, :, 0:128]
             edge = 127 if side == 0 else 0
             o = jnp.where(lane48 == l, pltpu.roll(tile, (l - edge) % 128, 1), o)
-        ko[side] = o
+        ko[side] = o.astype(BF16)
 
     def k_copy(side):
         return pltpu.make_async_remote_copy(
@@ -424,23 +419,13 @@
                     v = (up * sel[:, to : to + 256].astype(F32)).astype(BF16)
                     for s in range(S):
                         gc[s, x, y * 16 : y * 16 + 16, :] = v[s * 16 : s * 16 + 16]
-    @pl.when(owner)
-    def _():
-        p1_got.wait_recv()
-        r1[men] = wg[mine]
-        total = r1[0]
-        for n in range(1, 32):
-            total = total + r1[n]
-        r2[zc] = total
-        for n in range(1, 8):
-            p2(n).start()
-
     k_all.wait_recv()
     lane256 = iota((48, 256), 1)
+    edge_below, edge_above = rk[0].astype(F32), rk[1].astype(F32)
     for l in range(18):
         v = in32[l]
-        below = jnp.concatenate([pltpu.roll(rk[0], (0 - l) % 128, 1), jnp.zeros((48, 128), F32)], axis=1)
-        above = jnp.concatenate([jnp.zeros((48, 128), F32), pltpu.roll(rk[1], (127 - l) % 128, 1)], axis=1)
+        below = jnp.concatenate([pltpu.roll(edge_below, (0 - l) % 128, 1), jnp.zeros((48, 128), F32)], axis=1)
+        above = jnp.concatenate([jnp.zeros((48, 128), F32), pltpu.roll(edge_above, (127 - l) % 128, 1)], axis=1)
         lhs[l, 0:48, :] = jnp.where(lane256 == 0, below, pltpu.roll(v, 1, 1)).astype(BF16)
         lhs[l, 48:96, :] = v.astype(BF16)
         lhs[l, 96:144, :] = jnp.where(lane256 == 255, above, pltpu.roll(v, 255, 1)).astype(BF16)
@@ -467,10 +452,25 @@
         low_part = (t - mid.astype(F32)).astype(BF16)
         r = dot(jnp.concatenate([hi, mid, low_part], axis=0), qbuf[oy])
         w1 = w1 + (r[0:16] + r[16:32] + r[32:48])
-    ca[me_a, 0] = w1[0:8]
-    ca[me_a, 1] = w1[8:16]
-    for n in range(1, 8):
-        ta(n).start()
+    own1[0] = w1[0:8]
+    own1[1] = w1[8:16]
+    t1().start()
+
+    @pl.when(owner)
+    def _():
+        p1_got.wait_recv()
+        r1[men] = wg[mine]
+        total = r1[0]
+        for n in range(1, 32):
+            total = total + r1[n]
+        r2[zc] = total
+        for n in range(1, 8):
+            p2(n).start()
+
+    t1().wait_recv()
+    c2[chip] = own1[core] + c1[...]
+    for n in range(1, 16):
+        t2(n).start()
 
     @pl.when(owner)
     def _():
@@ -482,20 +482,16 @@
         for n in range(1, 16):
             p3(n).start()
 
-    ta_all.wait_recv()
-    total = ca[0]
+    t2_all.wait_recv()
+    total = c2[0]
+    for n in range(1, 16):
+        total = total + c2[n]
+    c3[core, zc] = total
     for n in range(1, 8):
-        total = total + ca[n]
-    cb[me_b] = total
-    for n in range(1, 4):
-        tb(n).start()
-    tb_all.wait_recv()
-    total = cb[0]
-    for n in range(1, 4):
-        total = total + cb[n]
-    cc[zc] = total
+        t3(n, dp).start()
+    t3(0, dp + 1 - 2 * core).start()
     for n in range(1, 8):
-        tc_(n).start()
+        t3(n, dp + 1 - 2 * core).start()
 
     @pl.when(owner)
     def _():
@@ -506,18 +502,19 @@
         p3_got_all.wait_recv()
 
     p4(core).start()
-    tc_all.wait_recv()
-    total = cc[0]
-    for n in range(1, 8):
-        total = total + cc[n]
-    fin[TILES] = total[0]
-    fin[TILES + 1] = total[1]
+    t3_all.wait_recv()
+    for half in range(2):
+        total = c3[half, 0]
+        for n in range(1, 8):
+            total = total + c3[half, n]
+        fin[TILES + half] = total
     p4(1 - core).wait_recv()
     fin_copy = pltpu.make_async_copy(fin, fin_h, o_sem.at[1])
     fin_copy.start()
 
-    for c in (gt_all, gx_all, gy_all, ix_all, iy_all, k_all, ta_all, tb_all, tc_all):
+    for c in (gt_all, gx_all, gy_all, ix_all, iy_all, k_all, t2_all, t3_all):
         c.wait_send()
+    t1().wait_send()
     p4(core).wait_send()
 
     @pl.when(owner)
@@ -583,8 +580,8 @@
             pltpu.VMEM((2, S, 4, 2048), BF16),
             pltpu.VMEM((2, S, 4, 1536), BF16),
             pltpu.VMEM((18, 48, 256), F32),
-            pltpu.VMEM((2, 48, 128), F32),
-            pltpu.VMEM((2, 48, 128), F32),
+            pltpu.VMEM((2, 48, 128), BF16),
+            pltpu.VMEM((2, 48, 128), BF16),
             pltpu.VMEM((18, 144, 256), BF16),
             pltpu.VMEM((48, 8192), BF16),
             pltpu.VMEM((S, 4, 128, 256), BF16),
@@ -594,9 +591,10 @@
             pltpu.VMEM((8, 8, 128), F32),
             pltpu.VMEM((TILES + 2, 8, 128), F32),
             pltpu.VMEM((3, 432, 128), BF16),
-            pltpu.VMEM((8, 2, 8, 128), F32),
-            pltpu.VMEM((4, 2, 8, 128), F32),
-            pltpu.VMEM((8, 2, 8, 128), F32),
+            pltpu.VMEM((2, 8, 128), F32),
+            pltpu.VMEM((8, 128), F32),
+            pltpu.VMEM((16, 8, 128), F32),
+            pltpu.VMEM((2, 8, 8, 128), F32),
             *[dma] * 12,
             *[dma] * 6,
             *[dma] * 8,

time: 47 us -> 46.8 us (level)
  no operation moved by 1% of the time
where the time goes in v4:
time: 46.8 us; the launch traced here: 46.7 us
  Pallas kernels  46.1 us (99%)
  between operations  0.64 us (1%)
    pallas_call x1, Pallas kernels, local(): pl.pallas_call(kernel, out_shape=(jax.ShapeDtypeStruct((48, 1024), BF16),...  44.3 us
    pallas_call x1, Pallas kernels, local(): pl.pallas_call(finish, out_shape=(jax.ShapeDtypeStruct((48, 1024), BF16),...  1.73 us

profile of v4, /device:TPU:1, one launch (start us, length us, event | category | flops | bytes accessed | tf_op | source)
XLA Modules:
  0.0 46.7 jit_solution(5923744508381636066)
XLA Ops:
  0.6 44.3 %whole.1 = (bf16[48,1024]{1,0:T(8,128)(2,1)}, f32[20,8,128]{2,1,0:T(8,128)}) custom-call(bf16[3,4,8192]{2,1,0:T(4,128)(2,1)} %bitcast.13, s32[48,8192]{1,0:T(8,128)} %bitcast.11, s32[48,1024]{1,0:T(8,128)} %bitcast.14, bf16[48,1024]{1,0:T(8,128)(2,1)} %bitcast.15, bf16[27,16,32]{2,1,0:T(8,128)(2,1)} %w_two_h.1, s32[96,1024]{1,0:T(8,128)} %bitcast.12, ...), custom_call_target="tpu_custom_call" | custom-call | tf_op jit(solution)/shard_map/whole/pallas_call | solution.py:551
  45.0 1.7 %finish.1 = (bf16[48,1024]{1,0:T(8,128)(2,1)}, f32[4,16,27]{2,1,0:T(8,128)}, f32[27,16,32]{2,1,0:T(8,128)}) custom-call(bf16[48,1024]{1,0:T(8,128)(2,1)} %get-tuple-element.8.gp, f32[20,8,128]{2,1,0:T(8,128)} %get-tuple-element.9.fin), custom_call_target="tpu_custom_call" | custom-call | tf_op jit(solution)/shard_map/finish/pallas_call | solution.py:617

commit v5 on v4

--- a/solution.py
+++ b/solution.py
@@ -43,10 +43,10 @@
     gp_h, fin_h,
     inp, mask_one, place_one, pooled, w_two, mask_two, place_two, grad_two, gp,
     mp, yb, tk, rx, ry, rt, z3, wp, pst, tbuf,
-    iyb, rix, riy, in32, ko, rk, lhs, sel, gc, acc1,
+    iyb, rix, riy, in32, rowsel, ysel, lhs, sel, gc, acc1,
     wg, r1, r2, fin, qbuf, own1, c1, c2, c3,
     gx_send, gx_recv, gy_send, gy_recv, gt_send, gt_recv,
-    ix_send, ix_recv, iy_send, iy_recv, k_send, k_recv,
+    ix_send, ix_recv, iy_send, iy_recv,
     s1_send, s1_recv, s2_send, s2_recv, s3_send, s3_recv,
     s4_send, s4_recv, ta_send, ta_recv, tb_send, tb_recv, tc_send, tc_recv,
     l_sem, o_sem,
@@ -134,7 +134,7 @@
         )
 
     gx_all, gy_all, gt_all = group(rx, gx_send, gx_recv), group(ry, gy_send, gy_recv), group(rt, gt_send, gt_recv)
-    ix_all, iy_all, k_all = group(rix, ix_send, ix_recv), group(riy, iy_send, iy_recv), group(rk, k_send, k_recv)
+    ix_all, iy_all = group(rix, ix_send, ix_recv), group(riy, iy_send, iy_recv)
     p1_got = group(r1.at[0:31], s1_send, s1_recv)
     p1_sent = group(wg.at[0 : TILES - 1], s1_send, s1_recv)
     p1_sent_all = group(wg, s1_send, s1_recv)
@@ -200,13 +200,28 @@
     yb[0] = jnp.where(low, m_f, pltpu.roll(p_f, 64, 1)).astype(BF16)
     yb[1] = jnp.where(low, pltpu.roll(m_f, 64, 1), p_f).astype(BF16)
     tr, tc = iota((16, 128), 0), iota((16, 128), 1)
-    tk[...] = jnp.zeros_like(tk)
+    loads[3].wait()
+    row4, lane4 = iota((4, 128), 0), iota((4, 128), 1)
     for side, edge in ((0, 63), (1, 0)):
         pick_m = one_hot((tr < 2) & (tc == tr * 64 + edge))
         pick_p = one_hot((tr >= 2) & (tr < 4) & (tc == (tr - 2) * 64 + edge))
-        tk[side, :, 0:96] = (dot(pick_m, m_b, NT) + dot(pick_p, p_b, NT)).astype(BF16)
-
-    loads[3].wait()
+        rows = jnp.concatenate(
+            [dot(pick_m, m_b, NT) + dot(pick_p, p_b, NT), jnp.zeros((16, 32), F32)], axis=1
+        )
+        for x in range(4):
+            line = jnp.zeros((1, 128), F32)
+            for s in range(S):
+                a = jnp.zeros((4, 128), F32)
+                for y in range(8):
+                    at = (x * 8 + y) * 256 + (128 if side == 0 else 0)
+                    v = inp[s, :, at : at + 128].astype(F32)
+                    v = v[:, 127:128] if side == 0 else v[:, 0:1]
+                    a = jnp.where(lane4 % 8 == y, jnp.broadcast_to(v, (4, 128)), a)
+                a = jnp.where(lane4 // 8 == s * 4 + row4, a, 0.0)
+                line = line + jnp.sum(a, axis=0, keepdims=True)
+            rows = jnp.where(tr == 4 + x, jnp.broadcast_to(line, (16, 128)), rows)
+        tk[side] = rows.astype(BF16)
+
     for q, y in ((0, 0), (1, 7)):
         for x in range(4):
             at = x * 2048 + y * 256
@@ -300,6 +315,24 @@
                     ok = (up == par1 + float(4 * dx + 2 * dy)) & (mask_one[:, to : to + 256] == 1)
                     sel[:, to : to + 256] = one_hot(ok)
 
+    in32[...] = jnp.zeros_like(in32)
+    for s in range(S):
+        for x in range(4):
+            for y in range(8):
+                at = (x * 8 + y) * 256
+                in32[s * 6 + x + 1, 4 * y + 4 : 4 * y + 8, :] = inp[s, :, at : at + 256].astype(F32)
+    sr, sc = iota((192, 288), 0), iota((192, 288), 1)
+    xp = sr % 32 % 6
+    from_i = jnp.where(xp == 0, 0, jnp.where(xp == 5, 2, 1))
+    from_x = jnp.where(xp == 0, 3, jnp.where(xp == 5, 0, xp - 1))
+    want = (from_i * 3 + (sr // 32) % 3) * 32 + (sr // 96) * 16 + 4 + from_x
+    rowsel[...] = one_hot((sc == want) & (sr % 32 < 18))
+    yr, yc = iota((48, 128), 0), iota((48, 128), 1)
+    same = (yr % 4 == (yc // 8) % 4) & (yc < 96)
+    ysel[0] = one_hot(same & (yr // 4 == 0) & (yc % 8 == 7))
+    ysel[1] = one_hot(same & (yr // 4 >= 1) & (yr // 4 <= 8) & (yc % 8 == yr // 4 - 1))
+    ysel[2] = one_hot(same & (yr // 4 == 9) & (yc % 8 == 0))
+
     fr, fc = iota((32, 768), 0), iota((32, 768), 1)
     f_in, f_mid, f_b = fc % 128, (fc // 128) % 2, fc // 256
     left = (f_b == 2) & (f_in == 0)
@@ -372,42 +405,6 @@
     gp_copy = pltpu.make_async_copy(gp, gp_h, o_sem.at[0])
     gp_copy.start()
 
-    for c in (ix_all, iy_all):
-        c.wait_recv()
-    in32[...] = jnp.zeros_like(in32)
-    for s in range(S):
-        for x in range(6):
-            for y in range(10):
-                if 1 <= y <= 8:
-                    if 1 <= x <= 4:
-                        at = ((x - 1) * 8 + y - 1) * 256
-                        v = inp[s, :, at : at + 256]
-                    else:
-                        at = (y - 1) * 256
-                        v = rix[0 if x == 0 else 1, s, :, at : at + 256]
-                else:
-                    v = riy[0 if y == 0 else 1, s, :, x * 256 : x * 256 + 256]
-                in32[s * 6 + x, 4 * y : 4 * y + 4, :] = v.astype(F32)
-    lane48 = iota((48, 128), 1)
-    for side in range(2):
-        o = jnp.zeros((48, 128), F32)
-        for l in range(18):
-            tile = in32[l, :, 128:256] if side == 0 else in32[l, :, 0:128]
-            edge = 127 if side == 0 else 0
-            o = jnp.where(lane48 == l, pltpu.roll(tile, (l - edge) % 128, 1), o)
-        ko[side] = o.astype(BF16)
-
-    def k_copy(side):
-        return pltpu.make_async_remote_copy(
-            src_ref=ko.at[side], dst_ref=rk.at[side],
-            send_sem=k_send, recv_sem=k_recv,
-            device_id=near(0, 0, 1 if side == 0 else -1), device_id_type=MESH,
-        )
-
-    k_copies = [k_copy(0), k_copy(1)]
-    for c in k_copies:
-        c.start()
-
     for hx in range(2):
         for hy in range(4):
             at = (hx * 4 + hy) * 128
@@ -419,9 +416,32 @@
                     v = (up * sel[:, to : to + 256].astype(F32)).astype(BF16)
                     for s in range(S):
                         gc[s, x, y * 16 : y * 16 + 16, :] = v[s * 16 : s * 16 + 16]
-    k_all.wait_recv()
+    picked = dot(rowsel[...], rt[...].reshape(288, 128))
+    picked = jnp.where(iota((192, 128), 1) // 32 == (iota((192, 128), 0) % 32) // 6, picked, 0.0).astype(BF16)
+    edges = []
+    for side in range(2):
+        e = jnp.zeros((48, 32), F32)
+        for j in range(3):
+            r = side * 96 + j * 32
+            e = e + dot(ysel[j], picked[r : r + 32], NT)
+        edges.append(jnp.concatenate([e, jnp.zeros((48, 96), F32)], axis=1))
+    edge_below, edge_above = edges
+
+    for c in (ix_all, iy_all):
+        c.wait_recv()
+    for s in range(S):
+        for x in range(6):
+            for y in range(10):
+                if 1 <= y <= 8:
+                    if 1 <= x <= 4:
+                        continue
+                    at = (y - 1) * 256
+                    v = rix[0 if x == 0 else 1, s, :, at : at + 256]
+                else:
+                    v = riy[0 if y == 0 else 1, s, :, x * 256 : x * 256 + 256]
+                in32[s * 6 + x, 4 * y : 4 * y + 4, :] = v.astype(F32)
+
     lane256 = iota((48, 256), 1)
-    edge_below, edge_above = rk[0].astype(F32), rk[1].astype(F32)
     for l in range(18):
         v = in32[l]
         below = jnp.concatenate([pltpu.roll(edge_below, (0 - l) % 128, 1), jnp.zeros((48, 128), F32)], axis=1)
@@ -512,7 +532,7 @@
     fin_copy = pltpu.make_async_copy(fin, fin_h, o_sem.at[1])
     fin_copy.start()
 
-    for c in (gt_all, gx_all, gy_all, ix_all, iy_all, k_all, t2_all, t3_all):
+    for c in (gt_all, gx_all, gy_all, ix_all, iy_all, t2_all, t3_all):
         c.wait_send()
     t1().wait_send()
     p4(core).wait_send()
@@ -580,8 +600,8 @@
             pltpu.VMEM((2, S, 4, 2048), BF16),
             pltpu.VMEM((2, S, 4, 1536), BF16),
             pltpu.VMEM((18, 48, 256), F32),
-            pltpu.VMEM((2, 48, 128), BF16),
-            pltpu.VMEM((2, 48, 128), BF16),
+            pltpu.VMEM((192, 288), BF16),
+            pltpu.VMEM((3, 48, 128), BF16),
             pltpu.VMEM((18, 144, 256), BF16),
             pltpu.VMEM((48, 8192), BF16),
             pltpu.VMEM((S, 4, 128, 256), BF16),
@@ -595,7 +615,7 @@
             pltpu.VMEM((8, 128), F32),
             pltpu.VMEM((16, 8, 128), F32),
             pltpu.VMEM((2, 8, 8, 128), F32),
-            *[dma] * 12,
+            *[dma] * 10,
             *[dma] * 6,
             *[dma] * 8,
             dma((8,)), dma((2,)),

time: 46.8 us -> 44.9 us (0.959)
  Pallas kernels: 46.1 us -> 44.1 us
    pallas_call x1, Pallas kernels: 44.3 us -> 42.4 us  [local(): pl.pallas_call(kernel, out_shape=(jax.ShapeDtypeStruct((48, 1024), BF16),...]
where the time goes in v5:
time: 44.9 us; the launch traced here: 44.8 us
  Pallas kernels  44.1 us (98%)
  between operations  0.64 us (1%)
    pallas_call x1, Pallas kernels, local(): pl.pallas_call(kernel, out_shape=(jax.ShapeDtypeStruct((48, 1024), BF16),...  42.4 us
    pallas_call x1, Pallas kernels, local(): pl.pallas_call(finish, out_shape=(jax.ShapeDtypeStruct((48, 1024), BF16),...  1.73 us

profile of v5, /device:TPU:1, one launch (start us, length us, event | category | flops | bytes accessed | tf_op | source)
XLA Modules:
  0.0 44.8 jit_solution(8957707969666304533)
XLA Ops:
  0.6 42.4 %whole.1 = (bf16[48,1024]{1,0:T(8,128)(2,1)}, f32[20,8,128]{2,1,0:T(8,128)}) custom-call(bf16[3,4,8192]{2,1,0:T(4,128)(2,1)} %bitcast.13, s32[48,8192]{1,0:T(8,128)} %bitcast.11, s32[48,1024]{1,0:T(8,128)} %bitcast.14, bf16[48,1024]{1,0:T(8,128)(2,1)} %bitcast.15, bf16[27,16,32]{2,1,0:T(8,128)(2,1)} %w_two_h.1, s32[96,1024]{1,0:T(8,128)} %bitcast.12, ...), custom_call_target="tpu_custom_call" | custom-call | tf_op jit(solution)/shard_map/whole/pallas_call | solution.py:571
  43.0 1.7 %finish.1 = (bf16[48,1024]{1,0:T(8,128)(2,1)}, f32[4,16,27]{2,1,0:T(8,128)}, f32[27,16,32]{2,1,0:T(8,128)}) custom-call(bf16[48,1024]{1,0:T(8,128)(2,1)} %get-tuple-element.8.gp, f32[20,8,128]{2,1,0:T(8,128)} %get-tuple-element.9.fin), custom_call_target="tpu_custom_call" | custom-call | tf_op jit(solution)/shard_map/finish/pallas_call | solution.py:637

commit v6 on v5

--- a/solution.py
+++ b/solution.py
@@ -10,7 +10,7 @@
 S = 3
 MESH = pl.DeviceIdType.MESH
 F32, BF16, I32 = jnp.float32, jnp.bfloat16, jnp.int32
-TILES = 18
+CHUNKS, ROWS = 16, 9
 TOTAL = 6291456
 NEIGHBOURS = [
     (di, dj, dk)
@@ -40,15 +40,15 @@
 
 def kernel(
     inp_h, mask_one_h, place_one_h, pooled_h, w_two_h, mask_two_h, place_two_h, grad_two_h,
-    gp_h, fin_h,
+    gp_h, fin_h, one_h,
     inp, mask_one, place_one, pooled, w_two, mask_two, place_two, grad_two, gp,
     mp, yb, tk, rx, ry, rt, z3, wp, pst, tbuf,
     iyb, rix, riy, in32, rowsel, ysel, lhs, sel, gc, acc1,
-    wg, r1, r2, fin, qbuf, own1, c1, c2, c3,
+    wg, r1, r2, fin, one, qbuf, own1, c1, c2, c3,
     gx_send, gx_recv, gy_send, gy_recv, gt_send, gt_recv,
     ix_send, ix_recv, iy_send, iy_recv,
     s1_send, s1_recv, s2_send, s2_recv, s3_send, s3_recv,
-    s4_send, s4_recv, ta_send, ta_recv, tb_send, tb_recv, tc_send, tc_recv,
+    ta_send, ta_recv, tb_send, tb_recv, tc_send, tc_recv,
     l_sem, o_sem,
 ):
     dp = lax.axis_index("dp")
@@ -58,8 +58,7 @@
     men = dp * 8 + t8
     core = dp % 2
     chip = (dp // 2) * 8 + t8
-    owner = ((core == 0) & (chip < 9)) | ((core == 1) & (chip >= 7))
-    mine = jnp.where(core == 0, chip, chip + 2)
+    owner = core == chip % 2
 
     def near(di, dj, dk):
         other = ((bi + di + 4) % 4) * 16 + ((bj + dj + 4) % 4) * 4 + (bk + dk + 4) % 4
@@ -74,36 +73,22 @@
     def twin():
         return {"dp": dp + 1 - 2 * core}
 
-    def owner_of(o):
-        n = o if o < 9 else o - 2
-        return {"dp": (n // 8) * 2 + (0 if o < 9 else 1), "space": zc * 8 + n % 8}
-
-    def is_mine(o):
-        return owner & (mine == o)
-
     def p1(o):
         return pltpu.make_async_remote_copy(
             src_ref=wg.at[o], dst_ref=r1.at[men], send_sem=s1_send, recv_sem=s1_recv,
-            device_id=owner_of(o), device_id_type=MESH,
-        )
-
-    def p2(n):
+            device_id={"dp": (o // 8) * 2 + o % 2, "space": zc * 8 + o % 8}, device_id_type=MESH,
+        )
+
+    def p2(n, to):
         return pltpu.make_async_remote_copy(
             src_ref=r2.at[zc], dst_ref=r2.at[zc], send_sem=s2_send, recv_sem=s2_recv,
-            device_id=column((zc + n) % 8), device_id_type=MESH,
+            device_id={"dp": to, "space": ((zc + n) % 8) * 8 + t8}, device_id_type=MESH,
         )
 
     def p3(n):
         return pltpu.make_async_remote_copy(
-            src_ref=fin.at[mine], dst_ref=fin.at[mine], send_sem=s3_send, recv_sem=s3_recv,
+            src_ref=fin.at[chip], dst_ref=fin.at[chip], send_sem=s3_send, recv_sem=s3_recv,
             device_id=chip_at((chip + n) % 16), device_id_type=MESH,
-        )
-
-    def p4(half):
-        nine = fin.at[pl.ds(half * 9, 9)]
-        return pltpu.make_async_remote_copy(
-            src_ref=nine, dst_ref=nine, send_sem=s4_send, recv_sem=s4_recv,
-            device_id=twin(), device_id_type=MESH,
         )
 
     def chip_at(n):
@@ -136,12 +121,12 @@
     gx_all, gy_all, gt_all = group(rx, gx_send, gx_recv), group(ry, gy_send, gy_recv), group(rt, gt_send, gt_recv)
     ix_all, iy_all = group(rix, ix_send, ix_recv), group(riy, iy_send, iy_recv)
     p1_got = group(r1.at[0:31], s1_send, s1_recv)
-    p1_sent = group(wg.at[0 : TILES - 1], s1_send, s1_recv)
+    p1_sent = group(wg.at[0 : CHUNKS - 1], s1_send, s1_recv)
     p1_sent_all = group(wg, s1_send, s1_recv)
-    p2_all = group(r2.at[0:7], s2_send, s2_recv)
-    p3_sent = group(r1.at[0:15], s3_send, s3_recv)
-    p3_got = group(fin.at[0:8], s3_send, s3_recv)
-    p3_got_all = group(fin.at[0:9], s3_send, s3_recv)
+    p2_sent = group(r1.at[0:15], s2_send, s2_recv)
+    p2_got = group(r2.at[0:7], s2_send, s2_recv)
+    p2_got_all = group(r2, s2_send, s2_recv)
+    p3_all = group(fin.at[0:15], s3_send, s3_recv)
     t2_all = group(c2.at[0:15], tb_send, tb_recv)
     t3_all = group(c2.at[0:15], tc_send, tc_recv)
 
@@ -383,10 +368,10 @@
     for s in range(S):
         w2 = w2 + dot(pst[s], z3[s], NT)
     w2 = jnp.concatenate([w2, jnp.zeros((144, 32), F32)], axis=1)
-    for i in range(TILES):
-        wg[i] = w2[i * 8 : i * 8 + 8]
-    for o in range(TILES):
-        @pl.when(~is_mine(o))
+    for i in range(CHUNKS):
+        wg[i] = w2[i * ROWS : i * ROWS + ROWS]
+    for o in range(CHUNKS):
+        @pl.when(~(owner & (chip == o)))
         def _():
             p1(o).start()
 
@@ -479,13 +464,15 @@
     @pl.when(owner)
     def _():
         p1_got.wait_recv()
-        r1[men] = wg[mine]
+        r1[men] = wg[chip]
         total = r1[0]
         for n in range(1, 32):
             total = total + r1[n]
         r2[zc] = total
         for n in range(1, 8):
-            p2(n).start()
+            p2(n, dp).start()
+            p2(n, dp + 1 - 2 * core).start()
+        p2(0, dp + 1 - 2 * core).start()
 
     t1().wait_recv()
     c2[chip] = own1[core] + c1[...]
@@ -494,13 +481,18 @@
 
     @pl.when(owner)
     def _():
-        p2_all.wait_recv()
-        total = r2[0]
-        for zz in range(1, 8):
-            total = total + r2[zz]
-        fin[mine] = total
-        for n in range(1, 16):
-            p3(n).start()
+        p2_got.wait_recv()
+
+    @pl.when(~owner)
+    def _():
+        p2_got_all.wait_recv()
+
+    total = r2[0]
+    for zz in range(1, 8):
+        total = total + r2[zz]
+    fin[chip] = total
+    for n in range(1, 16):
+        p3(n).start()
 
     t2_all.wait_recv()
     total = c2[0]
@@ -513,35 +505,26 @@
     for n in range(1, 8):
         t3(n, dp + 1 - 2 * core).start()
 
-    @pl.when(owner)
-    def _():
-        p3_got.wait_recv()
-
-    @pl.when(~owner)
-    def _():
-        p3_got_all.wait_recv()
-
-    p4(core).start()
+    p3_all.wait_recv()
+    fin_copy = pltpu.make_async_copy(fin, fin_h, o_sem.at[1])
+    fin_copy.start()
     t3_all.wait_recv()
     for half in range(2):
         total = c3[half, 0]
         for n in range(1, 8):
             total = total + c3[half, n]
-        fin[TILES + half] = total
-    p4(1 - core).wait_recv()
-    fin_copy = pltpu.make_async_copy(fin, fin_h, o_sem.at[1])
-    fin_copy.start()
-
-    for c in (gt_all, gx_all, gy_all, ix_all, iy_all, t2_all, t3_all):
+        one[half] = total
+    one_copy = pltpu.make_async_copy(one, one_h, o_sem.at[2])
+    one_copy.start()
+
+    for c in (gt_all, gx_all, gy_all, ix_all, iy_all, t2_all, t3_all, p3_all):
         c.wait_send()
     t1().wait_send()
-    p4(core).wait_send()
 
     @pl.when(owner)
     def _():
         p1_sent.wait_send()
-        p2_all.wait_send()
-        p3_sent.wait_send()
+        p2_sent.wait_send()
 
     @pl.when(~owner)
     def _():
@@ -549,17 +532,17 @@
 
     gp_copy.wait()
     fin_copy.wait()
-
-
-def finish(gp, fin, gp_out, w1_out, w2_out):
+    one_copy.wait()
+
+
+def finish(gp, fin, one, gp_out, w1_out, w2_out):
     gp_out[...] = gp[...]
+    v = jnp.concatenate([fin[n] for n in range(CHUNKS)], axis=0) * (float(TOTAL // 8) ** -0.5)
     for o9 in range(9):
-        for h in range(2):
-            v = fin[2 * o9 + h] * (float(TOTAL // 8) ** -0.5)
-            for b in range(3):
-                w2_out[o9 * 3 + b, h * 8 : h * 8 + 8, :] = v[:, b * 32 : b * 32 + 32]
+        for b in range(3):
+            w2_out[o9 * 3 + b] = v[o9 * 16 : o9 * 16 + 16, b * 32 : b * 32 + 32]
     for i in range(2):
-        v = fin[TILES + i] * (float(TOTAL) ** -0.5)
+        v = one[i] * (float(TOTAL) ** -0.5)
         for c in range(4):
             w1_out[c, i * 8 : i * 8 + 8, :] = v[:, c * 32 : c * 32 + 27]
 
@@ -568,14 +551,15 @@
     vm = pl.BlockSpec(memory_space=pltpu.VMEM)
     anywhere = pl.BlockSpec(memory_space=pl.ANY)
     dma = pltpu.SemaphoreType.DMA
-    gp, fin = pl.pallas_call(
+    gp, fin, one = pl.pallas_call(
         kernel,
         out_shape=(
             jax.ShapeDtypeStruct((48, 1024), BF16),
-            jax.ShapeDtypeStruct((TILES + 2, 8, 128), F32),
+            jax.ShapeDtypeStruct((CHUNKS, ROWS, 128), F32),
+            jax.ShapeDtypeStruct((2, 8, 128), F32),
         ),
         in_specs=[anywhere] * 8,
-        out_specs=(anywhere, anywhere),
+        out_specs=(anywhere, anywhere, anywhere),
         scratch_shapes=[
             pltpu.VMEM((S, 4, 8192), BF16),
             pltpu.VMEM((48, 8192), I32),
@@ -606,10 +590,11 @@
             pltpu.VMEM((48, 8192), BF16),
             pltpu.VMEM((S, 4, 128, 256), BF16),
             pltpu.VMEM((128, 432), F32),
-            pltpu.VMEM((TILES, 8, 128), F32),
-            pltpu.VMEM((32, 8, 128), F32),
-            pltpu.VMEM((8, 8, 128), F32),
-            pltpu.VMEM((TILES + 2, 8, 128), F32),
+            pltpu.VMEM((CHUNKS, ROWS, 128), F32),
+            pltpu.VMEM((32, ROWS, 128), F32),
+            pltpu.VMEM((8, ROWS, 128), F32),
+            pltpu.VMEM((CHUNKS, ROWS, 128), F32),
+            pltpu.VMEM((2, 8, 128), F32),
             pltpu.VMEM((3, 432, 128), BF16),
             pltpu.VMEM((2, 8, 128), F32),
             pltpu.VMEM((8, 128), F32),
@@ -617,8 +602,8 @@
             pltpu.VMEM((2, 8, 8, 128), F32),
             *[dma] * 10,
             *[dma] * 6,
-            *[dma] * 8,
-            dma((8,)), dma((2,)),
+            *[dma] * 6,
+            dma((8,)), dma((3,)),
         ],
         compiler_params=pltpu.CompilerParams(
             collective_id=0, has_side_effects=True, vmem_limit_bytes=56 * 1024 * 1024
@@ -641,10 +626,10 @@
             jax.ShapeDtypeStruct((4, 16, 27), F32),
             jax.ShapeDtypeStruct((27, 16, 32), F32),
         ),
-        in_specs=[vm, vm],
+        in_specs=[vm, vm, vm],
         out_specs=(vm, vm, vm),
         name="finish",
-    )(gp, fin)
+    )(gp, fin, one)
     return gp.reshape(S, 1, 16, 1024), w1.transpose(2, 0, 1), w2
 
 

time: 44.9 us -> 44.1 us (0.982)
  Pallas kernels: 44.1 us -> 43.4 us
    pallas_call x1, Pallas kernels: 42.4 us -> 41.6 us  [local(): pl.pallas_call(kernel, out_shape=(jax.ShapeDtypeStruct((48, 1024), BF16),...]
where the time goes in v6:
time: 44.1 us; the launch traced here: 44 us
  Pallas kernels  43.4 us (98%)
  between operations  0.64 us (1%)
    pallas_call x1, Pallas kernels, local(): pl.pallas_call(kernel, out_shape=(jax.ShapeDtypeStruct((48, 1024), BF16),...  41.6 us
    pallas_call x1, Pallas kernels, local(): pl.pallas_call(finish, out_shape=(jax.ShapeDtypeStruct((48, 1024), BF16),...  1.76 us

profile of v6, /device:TPU:1, one launch (start us, length us, event | category | flops | bytes accessed | tf_op | source)
XLA Modules:
  0.0 44.0 jit_solution(13581169360214473273)
XLA Ops:
  0.6 41.6 %whole.1 = (bf16[48,1024]{1,0:T(8,128)(2,1)}, f32[16,9,128]{2,1,0:T(8,128)}, f32[2,8,128]{2,1,0:T(8,128)}) custom-call(bf16[3,4,8192]{2,1,0:T(4,128)(2,1)} %bitcast.13, s32[48,8192]{1,0:T(8,128)} %bitcast.11, s32[48,1024]{1,0:T(8,128)} %bitcast.14, bf16[48,1024]{1,0:T(8,128)(2,1)} %bitcast.15, bf16[27,16,32]{2,1,0:T(8,128)(2,1)} %w_two_h.1, ...), custom_call_target="tpu_custom_call" | custom-call | tf_op jit(solution)/shard_map/whole/pallas_call | solution.py:554
  42.3 1.8 %finish.1 = (bf16[48,1024]{1,0:T(8,128)(2,1)}, f32[4,16,27]{2,1,0:T(8,128)}, f32[27,16,32]{2,1,0:T(8,128)}) custom-call(bf16[48,1024]{1,0:T(8,128)(2,1)} %get-tuple-element.9.gp, f32[16,9,128]{2,1,0:T(8,128)} %get-tuple-element.10.fin, f32[2,8,128]{2,1,0:T(8,128)} %get-tuple-element.11.one), custom_call_target="tpu_custom_call" | custom-call | tf_op jit(solution)/shard_map/finish/pallas_call | solution.py:622

commit v7 on v6

--- a/solution.py
+++ b/solution.py
@@ -333,7 +333,7 @@
     gt_all.wait_recv()
 
     def put(b, x, y, dx, dy, um, up):
-        v = jnp.where(up == dz[b] + float(4 * dx + 2 * dy), um, 0.0).astype(BF16)
+        v = jnp.where(up == (dz[b] + float(4 * dx + 2 * dy)).astype(BF16), um, jnp.zeros((), BF16))
         to = (x * 6 + y) * 128
         for s in range(S):
             z3[s, b * 32 : b * 32 + 32, to : to + 128] = v[s * 32 : s * 32 + 32]
@@ -348,8 +348,8 @@
             xs = {-1: [(0, 1)], 0: [(1, 0), (2, 1)], 1: [(3, 0)]}[di]
             if dj == 0:
                 ref = mp if di == 0 else rx.at[(di + 1) // 2]
-                um = dot(ref[0], e3) + dot(stack, f_m, TN)
-                up = dot(ref[1], e3) + dot(stack, f_p, TN)
+                um = (dot(ref[0], e3) + dot(stack, f_m, TN)).astype(BF16)
+                up = (dot(ref[1], e3) + dot(stack, f_p, TN)).astype(BF16)
                 for b in range(3):
                     for qy in range(2):
                         at = (b * 2 + qy) * 128
@@ -358,15 +358,24 @@
                                 put(b, x, 1 + 2 * qy + dy, dx, dy, um[:, at : at + 128], up[:, at : at + 128])
             else:
                 q = 1 if dj < 0 else 0
-                u = dot(ry[di + 1, (dj + 1) // 2], e3) + dot(stack, f_y[q], TN)
+                u = (dot(ry[di + 1, (dj + 1) // 2], e3) + dot(stack, f_y[q], TN)).astype(BF16)
                 for b in range(3):
                     at = b * 256
                     for x, dx in xs:
                         put(b, x, 0 if dj < 0 else 5, dx, q, u[:, at : at + 128], u[:, at + 128 : at + 256])
 
-    w2 = jnp.zeros((144, 96), F32)
-    for s in range(S):
-        w2 = w2 + dot(pst[s], z3[s], NT)
+    reach = [(96, 144), (48, 144), (0, 96), (0, 48)]
+    thirds = [jnp.zeros((48, 96), F32)] * 3
+    for x in range(4):
+        r0, r1_ = reach[x]
+        part = jnp.zeros((r1_ - r0, 96), F32)
+        for s in range(S):
+            part = part + dot(
+                pst[s, r0:r1_, x * 768 : x * 768 + 768], z3[s, :, x * 768 : x * 768 + 768], NT
+            )
+        for r in range(r0, r1_, 48):
+            thirds[r // 48] = thirds[r // 48] + part[r - r0 : r - r0 + 48]
+    w2 = jnp.concatenate(thirds, axis=0)
     w2 = jnp.concatenate([w2, jnp.zeros((144, 32), F32)], axis=1)
     for i in range(CHUNKS):
         wg[i] = w2[i * ROWS : i * ROWS + ROWS]
@@ -377,7 +386,8 @@
 
     for s in range(S):
         for x in range(4):
-            tbuf[:, x * 768 : x * 768 + 768] = dot(wp[...], z3[s, :, x * 768 : x * 768 + 768])
+            r0, r1_ = reach[x]
+            tbuf[r0:r1_, x * 768 : x * 768 + 768] = dot(wp[r0:r1_, :], z3[s, :, x * 768 : x * 768 + 768])
         for x in range(2):
             for y in range(4):
                 a = jnp.zeros((16, 128), F32)
@@ -412,28 +422,28 @@
         edges.append(jnp.concatenate([e, jnp.zeros((48, 96), F32)], axis=1))
     edge_below, edge_above = edges
 
-    for c in (ix_all, iy_all):
-        c.wait_recv()
-    for s in range(S):
-        for x in range(6):
+    lane256 = iota((48, 256), 1)
+    beside = jnp.zeros((48, 128), F32)
+    iy_all.wait_recv()
+    for x in (1, 2, 3, 4, 0, 5):
+        if x == 0:
+            ix_all.wait_recv()
+        for s in range(S):
+            l = s * 6 + x
             for y in range(10):
-                if 1 <= y <= 8:
-                    if 1 <= x <= 4:
-                        continue
-                    at = (y - 1) * 256
-                    v = rix[0 if x == 0 else 1, s, :, at : at + 256]
+                if y in (0, 9):
+                    v = riy[0 if y == 0 else 1, s, :, x * 256 : x * 256 + 256]
+                elif x in (0, 5):
+                    v = rix[0 if x == 0 else 1, s, :, (y - 1) * 256 : y * 256]
                 else:
-                    v = riy[0 if y == 0 else 1, s, :, x * 256 : x * 256 + 256]
-                in32[s * 6 + x, 4 * y : 4 * y + 4, :] = v.astype(F32)
-
-    lane256 = iota((48, 256), 1)
-    for l in range(18):
-        v = in32[l]
-        below = jnp.concatenate([pltpu.roll(edge_below, (0 - l) % 128, 1), jnp.zeros((48, 128), F32)], axis=1)
-        above = jnp.concatenate([jnp.zeros((48, 128), F32), pltpu.roll(edge_above, (127 - l) % 128, 1)], axis=1)
-        lhs[l, 0:48, :] = jnp.where(lane256 == 0, below, pltpu.roll(v, 1, 1)).astype(BF16)
-        lhs[l, 48:96, :] = v.astype(BF16)
-        lhs[l, 96:144, :] = jnp.where(lane256 == 255, above, pltpu.roll(v, 255, 1)).astype(BF16)
+                    continue
+                in32[l, 4 * y : 4 * y + 4, :] = v.astype(F32)
+            v = in32[l]
+            below = jnp.concatenate([pltpu.roll(edge_below, (0 - l) % 128, 1), beside], axis=1)
+            above = jnp.concatenate([beside, pltpu.roll(edge_above, (127 - l) % 128, 1)], axis=1)
+            lhs[l, 0:48, :] = jnp.where(lane256 == 0, below, pltpu.roll(v, 1, 1)).astype(BF16)
+            lhs[l, 48:96, :] = v.astype(BF16)
+            lhs[l, 96:144, :] = jnp.where(lane256 == 255, above, pltpu.roll(v, 255, 1)).astype(BF16)
 
     a1 = jnp.zeros((128, 432), F32)
     for s in range(S):

time: 44.1 us -> 43.8 us (level)
  no operation moved by 1% of the time
where the time goes in v7:
time: 43.8 us; the launch traced here: 43.7 us
  Pallas kernels  43.1 us (98%)
  between operations  0.64 us (1%)
    pallas_call x1, Pallas kernels, local(): pl.pallas_call(kernel, out_shape=(jax.ShapeDtypeStruct((48, 1024), BF16),...  41.3 us
    pallas_call x1, Pallas kernels, local(): pl.pallas_call(finish, out_shape=(jax.ShapeDtypeStruct((48, 1024), BF16),...  1.76 us

profile of v7, /device:TPU:1, one launch (start us, length us, event | category | flops | bytes accessed | tf_op | source)
XLA Modules:
  0.0 43.7 jit_solution(532064546368362546)
XLA Ops:
  0.6 41.3 %whole.1 = (bf16[48,1024]{1,0:T(8,128)(2,1)}, f32[16,9,128]{2,1,0:T(8,128)}, f32[2,8,128]{2,1,0:T(8,128)}) custom-call(bf16[3,4,8192]{2,1,0:T(4,128)(2,1)} %bitcast.13, s32[48,8192]{1,0:T(8,128)} %bitcast.11, s32[48,1024]{1,0:T(8,128)} %bitcast.14, bf16[48,1024]{1,0:T(8,128)(2,1)} %bitcast.15, bf16[27,16,32]{2,1,0:T(8,128)(2,1)} %w_two_h.1, ...), custom_call_target="tpu_custom_call" | custom-call | tf_op jit(solution)/shard_map/whole/pallas_call | solution.py:564
  41.9 1.8 %finish.1 = (bf16[48,1024]{1,0:T(8,128)(2,1)}, f32[4,16,27]{2,1,0:T(8,128)}, f32[27,16,32]{2,1,0:T(8,128)}) custom-call(bf16[48,1024]{1,0:T(8,128)(2,1)} %get-tuple-element.9.gp, f32[16,9,128]{2,1,0:T(8,128)} %get-tuple-element.10.fin, f32[2,8,128]{2,1,0:T(8,128)} %get-tuple-element.11.one), custom_call_target="tpu_custom_call" | custom-call | tf_op jit(solution)/shard_map/finish/pallas_call | solution.py:632
